TPU v7x, 32 devices: a whole 2x2x4 slice. The times are simulated.
32 devices in a mesh: dp: 4 (over y, x), tensor: 8 (over z, core).
Axes of the slice: x: 2, y: 2, z: 4, core: 2. Of those that a mesh axis runs over, the one named last changes fastest.
Arguments:
- tokens: bfloat16 [8192, 1024], P(('dp', 'tensor')), may hold values from -6 to 6
- class_embed: float32 [4, 6, 1024], P('dp', None, 'tensor'), may hold values from -6 to 6
- item_lengths: int32 [4, 6], P('dp'), may hold values from 1 to 680, 2048 in all within a row
- token_codes: int32 [8192], P(('dp', 'tensor')), may hold values from 0 to 4095
- ada_weight: bfloat16 [1024, 6144], P('tensor'), may hold values from -0.375 to 0.375
- ada_bias: float32 [6144], replicated, may hold values from -4 to 4
- qkv_weight: bfloat16 [1024, 3, 1024], P(None, None, 'tensor'), may hold values from -0.1875 to 0.1875
- query_bias: float32 [1024], P('tensor'), may hold values from -6 to 6
- value_bias: float32 [1024], P('tensor'), may hold values from -6 to 6
- head_scale: float32 [16], P('tensor'), may hold values from 2 to 2.8
- proj_weight: bfloat16 [1024, 1024], P('tensor'), may hold values from -0.1875 to 0.1875
- proj_bias: float32 [1024], replicated, may hold values from -4 to 4
- up_weight: bfloat16 [1024, 4096], P(None, 'tensor'), may hold values from -0.1875 to 0.1875
- up_bias: float32 [4096], replicated, may hold values from -6 to 6
- down_weight: bfloat16 [4096, 1024], P('tensor'), may hold values from -0.09375 to 0.09375
- down_bias: float32 [1024], replicated, may hold values from -4 to 4
- out_grad: bfloat16 [8192, 1024], P(('dp', 'tensor')), may hold values from -6 to 6
Outputs:
- layer_out: bfloat16 [8192, 1024], P(('dp', 'tensor'))
- tokens_grad: float32 [8192, 1024], P(('dp', 'tensor'))
- embed_grad: float32 [4, 6, 1024], P('dp', None, 'tensor')
- adaw_grad: float32 [1024, 6144], P('tensor')
- adab_grad: float32 [6144], replicated
- qkvw_grad: float32 [1024, 3, 1024], P(None, None, 'tensor')
- qbias_grad: float32 [1024], P('tensor')
- vbias_grad: float32 [1024], P('tensor')
- hscale_grad: float32 [16], P('tensor')
- projw_grad: float32 [1024, 1024], P('tensor')
- projb_grad: float32 [1024], replicated
- upw_grad: float32 [1024, 4096], P(None, 'tensor')
- upb_grad: float32 [4096], P('tensor')
- downw_grad: float32 [4096, 1024], P('tensor')
- downb_grad: float32 [1024], replicated
- code_hist: float32 [4096], replicated
Inputs may be any that keep to these rules, and one draw needn't show every extreme that they name: `item_lengths`: in each row the 6 lengths sum to 2048, and one of them is exactly 680.
All inputs are finite; a program needn't handle non-finite values.
Results may differ from a plain program's by a relative error of at most 0.028.
Values may be sent and summed in bfloat16 or wider, within the bound.
A program may use at most 128 MiB of HBM per device.

v0:
```python
import functools

import jax
import jax.numpy as jnp
from jax import lax
from jax.experimental import pallas as pl
from jax.experimental.pallas import tpu as pltpu
from jax.sharding import PartitionSpec as P

HEAD = 64
NBINS = 4096
ROW_LEN = 2048
SEGS = 6
D = 1024
ITEM_MAX = 680
CORES = 2
LANES = 128

epsilon = 1e-06
scale_starts = (1, 5, 14, 30, 55, 91, 155, 255, 424)
AHEAD = ITEM_MAX - scale_starts[-1] - 1
BEHIND = ITEM_MAX - 1
highest = lax.Precision.HIGHEST
f32 = jnp.float32
bf16 = jnp.bfloat16
MESH = pl.DeviceIdType.MESH
VMEM_LIMIT = 56 << 20


def dot(a, b, ca=1, cb=0, precision=None):
    return lax.dot_general(
        a, b, (((ca,), (cb,)), ((), ())), preferred_element_type=f32, precision=precision
    )


def item_layout(lengths):
    ends = jnp.cumsum(lengths, dtype=jnp.int32)
    begin = ends - lengths
    position = jnp.arange(ROW_LEN, dtype=jnp.int32)
    segment = jnp.sum((position[:, None] >= ends[None, :]).astype(jnp.int32), axis=1)
    chosen = segment[:, None] == jnp.arange(SEGS, dtype=jnp.int32)[None, :]
    inside = position - jnp.sum(jnp.where(chosen, begin[None, :], 0), axis=1)
    scale_ids = jnp.zeros_like(inside)
    for threshold in scale_starts:
        scale_ids = scale_ids + (inside >= threshold).astype(jnp.int32)
    return segment, scale_ids


def greet(peers):
    barrier = pltpu.get_barrier_semaphore()
    for p in peers:
        pl.semaphore_signal(barrier, inc=1, device_id=p, device_id_type=MESH)
    pl.semaphore_wait(barrier, len(peers))


def remote(src, dst, send, recv, to):
    return pltpu.make_async_remote_copy(
        src_ref=src,
        dst_ref=dst,
        send_sem=send,
        recv_sem=recv,
        device_id=to,
        device_id_type=MESH,
    )


class Place:
    def __init__(self, n, nd):
        self.n, self.nd, self.nz = n, nd, n // CORES
        self.dp, self.me = lax.axis_index("dp"), lax.axis_index("tensor")
        self.z, self.core = self.me // CORES, lax.rem(self.me, CORES)
        self.orders = orders_of(nd)
        self.far = sorted(range(1, self.nz), key=lambda o: min(o, self.nz - o))

    def chip(self, step):
        return lax.rem(self.z + step + self.nz, self.nz)

    def on_chip(self, step):
        return (self.dp, self.chip(step) * CORES + self.core)

    def twin(self):
        return (self.dp, self.z * CORES + 1 - self.core)

    def flip(self, bit):
        return (self.dp ^ (1 << bit), self.me)

    def line(self):
        return [(self.dp, lax.rem(self.me + o, self.n)) for o in range(1, self.n)]

    def greet_all(self):
        greet(self.line() + [self.flip(b) for b in range(bits_of(self.nd))])


def bits_of(nd):
    return nd.bit_length() - 1


def orders_of(nd):
    m = bits_of(nd)
    return [list(range(m)), [(m // 2 + i) % m for i in range(m)]]


def spread_plan(order):
    plan = [(0, list(order))]
    for i, bit in enumerate(order):
        plan += [(rel | (1 << bit), list(order[i + 1 :])) for rel, _ in list(plan)]
    return plan


class Spread:
    def __init__(self, place, ref_of, send, recv):
        self.place, self.ref_of, self.send, self.recv = place, ref_of, send, recv
        self.levels = bits_of(place.nd)

    def sends(self, part, rel, bits):
        p = self.place
        ref = self.ref_of(part, p.dp ^ rel)
        for bit in bits:
            to = rel | (1 << bit)
            yield remote(ref, ref, self.send.at[part, to], self.recv.at[part, to], p.flip(bit))

    def arrived(self, level):
        for part, order in enumerate(self.place.orders):
            for rel, bits in spread_plan(order):
                if rel and len(order) - 1 - len(bits) == level:
                    yield part, rel, bits

    def begin(self):
        for part, order in enumerate(self.place.orders):
            for c in self.sends(part, 0, order):
                c.start()

    def step(self, level):
        p = self.place
        for part, rel, bits in self.arrived(level):
            ref = self.ref_of(part, p.dp ^ rel)
            remote(
                ref, ref, self.send.at[part, rel], self.recv.at[part, rel], p.flip(0)
            ).wait_recv()
            for c in self.sends(part, rel, bits):
                c.start()

    def end(self):
        for part, order in enumerate(self.place.orders):
            for rel, bits in spread_plan(order):
                for c in self.sends(part, rel, bits):
                    c.wait_send()


class Line:
    def __init__(self, place, own, ref_of, send, recv):
        self.p, self.own, self.ref_of, self.send, self.recv = place, own, ref_of, send, recv
        self.ways = (1, -1)

    def inside(self, z):
        return (z >= 0) & (z < self.p.nz)

    def source(self, w, step):
        z = self.p.z - self.ways[w] * step
        return jnp.clip(z, 0, self.p.nz - 1), self.inside(z)

    def copy(self, w, step):
        p = self.p
        to = p.z + self.ways[w]
        chip, have = self.source(w, step - 1)
        src = self.own if step == 1 else self.ref_of(chip)
        c = remote(
            src,
            self.ref_of(chip),
            self.send.at[w, step],
            self.recv.at[w, step],
            (p.dp, jnp.clip(to, 0, p.nz - 1) * CORES + p.core),
        )
        return c, have & self.inside(to)

    def start(self, step=1):
        for w in range(2):
            c, do = self.copy(w, step)
            pl.when(do)(c.start)

    def got(self, step, then):
        for w in range(2):
            chip, have = self.source(w, step)
            to = self.p.z + self.ways[w]
            ref = self.ref_of(chip)
            wait = remote(
                ref, ref, self.send.at[w, step], self.recv.at[w, step], self.p.twin()
            )
            on, more = None, None
            if step + 1 < self.p.nz:
                on, more = self.copy(w, step + 1)

            @pl.when(have)
            def _():
                wait.wait_recv()
                if on is not None:
                    pl.when(more)(on.start)
                then(w, chip)

    def each(self, step, do):
        for w in range(2):
            chip, have = self.source(w, step)
            pl.when(have)(functools.partial(do, w, chip))

    def end(self):
        for step in range(1, self.p.nz):
            for w in range(2):
                c, do = self.copy(w, step)
                pl.when(do)(c.wait_send)


def picks_of(seg):
    return (seg == lax.broadcasted_iota(jnp.int32, (seg.shape[0], 8), 1)).astype(bf16)


def two(x):
    high = x.astype(bf16)
    return high, (x - high.astype(f32)).astype(bf16)


def per_token(picks, table):
    high, low = two(table)
    return dot(picks, high) + dot(picks, low)


def per_item(picks, values):
    high, low = two(values)
    return dot(picks, high, 0, 0) + dot(picks, low, 0, 0)


def norm_parts(values):
    centred = values - jnp.mean(values, axis=-1, keepdims=True)
    rstd = lax.rsqrt(jnp.mean(centred * centred, axis=-1, keepdims=True) + epsilon)
    return centred * rstd, rstd


def norm_back(normal, rstd, scaled):
    return rstd * (
        scaled
        - jnp.mean(scaled, axis=-1, keepdims=True)
        - normal * jnp.mean(scaled * normal, axis=-1, keepdims=True)
    )


GAMMA_ONE, GAMMA_TWO, SCALE_ONE, SCALE_TWO, SHIFT_ONE, SHIFT_TWO = range(6)


def half_lanes(rows):
    return lax.broadcasted_iota(jnp.int32, (rows, LANES), 1) < HEAD


def half_sums(x):
    low = half_lanes(x.shape[0])
    a = jnp.sum(jnp.where(low, x, 0.0), axis=1, keepdims=True)
    b = jnp.sum(jnp.where(low, 0.0, x), axis=1, keepdims=True)
    return jnp.where(low, a, b)


def one_half(x, h):
    low = half_lanes(x.shape[0])
    return jnp.where(low if h == 0 else jnp.logical_not(low), x, jnp.zeros_like(x))


def back_body(
    block, nq, nk, need_ref, q_ref, k_ref, v_ref, g_ref, o_ref, l_ref, ehs_ref, lo_ref, hi_ref,
    e_ref, n_ref, a_ref, w_ref, dw_ref, gn_ref, sums_ref, ku, dk, dv, dq, gqs, gkv,
):
    t = nq * block
    k = k_ref[0]
    rk = lax.rsqrt(half_sums(k * k) + epsilon)
    ku[...] = (k * rk).astype(bf16)
    dk[...] = jnp.zeros_like(dk)
    dv[...] = jnp.zeros_like(dv)
    ehs = ehs_ref[0]
    qsum = jnp.zeros((1, LANES), f32)
    hsum = jnp.zeros((1, LANES), f32)
    for qi in range(nq):
        rows = pl.ds(qi * block, block)
        q = q_ref[0, rows, :]
        rq = lax.rsqrt(half_sums(q * q) + epsilon)
        qhat = q * rq
        qu = (qhat * ehs).astype(bf16)
        qs = [one_half(qu, h) for h in range(2)]
        g = g_ref[0, rows, :]
        gs = [one_half(g, h) for h in range(2)]
        turned = (g.astype(f32) * o_ref[0, rows, :].astype(f32)).T
        deltas = [
            jnp.sum(turned[:HEAD], axis=0, keepdims=True),
            jnp.sum(turned[HEAD:], axis=0, keepdims=True),
        ]
        invs = [1.0 / l_ref[0, h : h + 1, rows] for h in range(2)]
        lo, hi = lo_ref[:, rows], hi_ref[:, rows]
        dq[...] = jnp.zeros_like(dq)
        for ki in range(nk):

            @pl.when(need_ref[qi * nk + ki] > 0)
            def _():
                cols = pl.ds(ki * block, block)
                e = e_ref[cols, :]
                allowed = (e >= lo) & (e <= hi)
                kb, vb = ku[cols, :], v_ref[0, cols, :]
                for h in range(2):
                    s = dot(kb, qs[h], 1, 1)
                    p = jnp.where(allowed, jnp.exp(s) * invs[h], 0.0)
                    dp = dot(vb, gs[h], 1, 1)
                    ds = (p * (dp - deltas[h])).astype(bf16)
                    dv[cols, :] += dot(p.astype(bf16), gs[h])
                    dk[cols, :] += dot(ds, qs[h])
                    dq[...] += dot(ds, one_half(kb, h), 0, 0)

        d = dq[...]
        hsum = hsum + jnp.sum(d * qhat * ehs, axis=0, keepdims=True)
        gq = (ehs * rq * (d - qhat * half_sums(qhat * d))).astype(bf16)
        gqs[rows, :] = gq
        qsum = qsum + jnp.sum(gq.astype(f32), axis=0, keepdims=True)
    khat = k * rk
    d = dk[...]
    gkv[:, :LANES] = (rk * (d - khat * half_sums(khat * d))).astype(bf16)
    gv = dv[...].astype(bf16)
    gkv[:, LANES:] = gv
    sums_ref[...] = jnp.zeros_like(sums_ref)
    sums_ref[0, 0:1, :] = qsum
    sums_ref[0, 1:2, :] = jnp.sum(gv.astype(f32), axis=0, keepdims=True)
    sums_ref[0, 2:3, :] = hsum
    dw_ref[0, :LANES, :] = dot(gqs[...], n_ref[:t, :], 0, 0).astype(bf16)
    dw_ref[0, LANES : 3 * LANES, :] = dot(gkv[...], n_ref[...], 0, 0).astype(bf16)
    dw_ref[0, 3 * LANES :, :] = dot(o_ref[0], a_ref[...], 0, 0).astype(bf16)

    @pl.when(pl.program_id(0) == 0)
    def _():
        gn_ref[...] = jnp.zeros_like(gn_ref)

    gn_ref[...] += dot(gkv[...], w_ref[0, LANES : 3 * LANES, :])
    gn_ref[:t, :] += dot(gqs[...], w_ref[0, :LANES, :])


def attend_back(need, q, k, v, g, o, l, ehs, lo_row, hi_row, e_col, normed, wide, weights, block):
    pairs, t, _ = q.shape
    w = k.shape[1]
    nq, nk = t // block, w // block
    slot = lambda rows: pl.BlockSpec((1, rows, LANES), lambda i, *_: (i, 0, 0))
    whole = lambda *shape: pl.BlockSpec(shape, lambda i, *_: (0,) * len(shape))
    return pl.pallas_call(
        functools.partial(back_body, block, nq, nk),
        grid_spec=pltpu.PrefetchScalarGridSpec(
            num_scalar_prefetch=1,
            grid=(pairs,),
            in_specs=[
                slot(t),
                slot(w),
                slot(w),
                slot(t),
                slot(t),
                pl.BlockSpec((1, 8, t), lambda i, *_: (i, 0, 0)),
                slot(1),
                whole(1, t),
                whole(1, t),
                whole(w, 1),
                whole(w, D),
                whole(t, D),
                pl.BlockSpec((1, 4 * LANES, D), lambda i, *_: (i, 0, 0)),
            ],
            out_specs=[
                pl.BlockSpec((1, 4 * LANES, D), lambda i, *_: (i, 0, 0)),
                whole(w, D),
                slot(8),
            ],
            scratch_shapes=[
                pltpu.VMEM((w, LANES), bf16),
                pltpu.VMEM((w, LANES), f32),
                pltpu.VMEM((w, LANES), f32),
                pltpu.VMEM((block, LANES), f32),
                pltpu.VMEM((t, LANES), bf16),
                pltpu.VMEM((w, 2 * LANES), bf16),
            ],
        ),
        out_shape=[
            jax.ShapeDtypeStruct((pairs, 4 * LANES, D), bf16),
            jax.ShapeDtypeStruct((w, D), f32),
            jax.ShapeDtypeStruct((pairs, 8, LANES), f32),
        ],
        compiler_params=pltpu.CompilerParams(vmem_limit_bytes=VMEM_LIMIT),
        name="attend_back",
    )(need, q, k, v, g, o, l, ehs, lo_row, hi_row, e_col, normed, wide, weights)


def ranks_at(lengths_ref, owner, tok, shape, axis):
    place = jnp.maximum(owner, 0) * tok + lax.broadcasted_iota(jnp.int32, shape, axis)
    item = jnp.zeros(shape, jnp.int32)
    begin = jnp.zeros(shape, jnp.int32)
    end = jnp.int32(0)
    for i in range(SEGS):
        end = end + lengths_ref[i]
        past = place >= end
        item = item + past.astype(jnp.int32)
        begin = jnp.where(past, end, begin)
    rank = item * 16
    for threshold in scale_starts:
        rank = rank + (place - begin >= threshold).astype(jnp.int32)
    there = owner >= 0
    return item, jnp.where(there, rank, -1)


def owners_of(p, steps):
    owners = []
    for s in [(0, 0)] + list(steps):
        for flip in range(CORES):
            c = p.core ^ flip
            far = [p.nz if v is None else v for v in s]
            chip = p.z - jnp.where(c == 0, far[0], far[1])
            owners.append(jnp.where((chip >= 0) & (chip < p.nz), chip * CORES + c, -1))
    return owners


def seen_lists(steps, tok):
    lists = []
    for qi in range(CORES):
        seen = set()
        for c in range(CORES):
            query = c ^ qi
            for i, s in enumerate([(0, 0)] + list(steps)):
                for flip in range(CORES):
                    owner = c ^ flip
                    if s[owner] is None:
                        continue
                    off = owner - s[owner] * CORES - query
                    near = off == 0
                    behind = off < 0 and (-off - 1) * tok + 1 <= BEHIND
                    ahead = off > 0 and (off - 1) * tok + 1 <= AHEAD
                    if near or behind or ahead:
                        seen.add(2 * i + flip)
        lists.append(seen)
    both = sorted(lists[0] & lists[1])
    rest = [sorted(v - set(both)) for v in lists]
    size = max(len(r) for r in rest)
    for r in rest:
        spare = [b for b in range(2 * len(steps) + 2) if b not in both and b not in r]
        r += spare[: size - len(r)]
    return [both + rest[0], both + rest[1]]


def block_at(lists, qi, j):
    a, b = lists[0][j], lists[1][j]
    return a if a == b else jnp.where(qi == 0, a, b)


def forward_body(
    n, nd, steps, width, len_ref, tok_ref, grad_ref, part_ref, extra_ref, abias_ref, pb_ref,
    apack_ref, mpack_ref,
    n_out, q_out, k_out, v_out, o_ref, l_ref, wa_out, wm_ref, branch_ref, resid_ref, nwide_ref,
    gwide_ref, mod_ref, ehs_ref,
    win, wa, modc, held, normed, qv, kv, vv, qb, vb, masks, ku, v0, v1, theirs, got,
    s1, r1, s2, r2, ts, tr, cs, cr, azs, azr, mzs, mzr, local_sem, out_sem, das, dar, dms, dmr,
    ms, mr,
):
    p = Place(n, nd)
    nz, tok = p.nz, grad_ref.shape[0]
    rounds = len(steps)
    blocks = 2 * rounds + 2
    pairs = qv.shape[0]
    merge = LANES // width
    rows = 4 * width // nd
    half = D // 2
    chunk = modc.shape[2]
    owners = owners_of(p, steps)
    p.greet_all()
    line = p.line()

    a_at = lambda chip, d: wa.at[chip, pl.ds(d * rows, rows)]
    mine = pl.ds(p.dp * rows, rows)
    al = Line(p, apack_ref.at[mine], lambda chip: wa.at[chip, mine], azs, azr)
    ml = Line(p, mpack_ref.at[:, p.dp], lambda chip: wm_ref.at[chip, :, p.dp], mzs, mzr)

    def a_spread(w, step, chip):
        return Spread(
            p,
            lambda part, d: wa.at[chip, pl.ds(d * rows, rows), pl.ds(part * half, half)],
            das.at[w, step],
            dar.at[w, step],
        )

    def m_spread(w, step, chip):
        return Spread(
            p, lambda part, d: wm_ref.at[chip, part, d], dms.at[w, step], dmr.at[w, step]
        )

    al.start()
    owns = [
        pltpu.make_async_copy(tok_ref, win.at[0], local_sem.at[0]),
        pltpu.make_async_copy(apack_ref, wa.at[p.z], local_sem.at[1]),
        pltpu.make_async_copy(mpack_ref, wm_ref.at[p.z], local_sem.at[2]),
    ]
    for c in owns:
        c.start()
    sums = [
        remote(part_ref.at[q[1]], held.at[o], s1.at[o], r1.at[o], q) for o, q in enumerate(line)
    ]
    for c in sums:
        c.start()
    twins = [
        remote(tok_ref if i == 0 else win.at[2 * i], win.at[2 * i + 1], cs.at[i], cr.at[i], p.twin())
        for i in range(rounds + 1)
    ]
    twins[0].start()
    for c in sums:
        c.wait()
    total = part_ref[p.me] + extra_ref[...] + abias_ref[p.me]
    for o in range(n - 1):
        total = total + held[o]
    modc[p.me] = total
    sums = [
        remote(modc.at[p.me], modc.at[p.me], s2.at[o], r2.at[o], q) for o, q in enumerate(line)
    ]
    for c in sums:
        c.start()
    moves = []
    for i, per_core in enumerate(steps):
        for c, step in enumerate(per_core):
            if step is None:
                continue
            go = (p.core == c) & (p.z + step >= 0) & (p.z + step < nz)
            have = (p.core == c) & (p.z - step >= 0) & (p.z - step < nz)
            to = (p.dp, jnp.clip(p.z + step, 0, nz - 1) * CORES + p.core)
            moves.append((i, go, have, remote(tok_ref, win.at[2 * i + 2], ts.at[i, c], tr.at[i, c], to)))
    al.got(1, lambda w, chip: a_spread(w, 1, chip).begin())
    for i, go, have, copy in moves:
        pl.when(go)(copy.start)
    for step in range(2, nz):
        al.got(step, lambda w, chip: a_spread(w, step, chip).begin())
    ml.start()

    for c in sums:
        c.wait()
    for j in range(n):
        mod_ref[:, j * chunk : (j + 1) * chunk] = modc[j]
    table = lambda which: mod_ref[:, which * D : (which + 1) * D]
    for s in range(pairs):
        parts = []
        for i in range(merge):
            r = modc[(s * merge + i) * CORES + p.core, SEGS : SEGS + 1, :]
            parts.append([r[:, k * width : (k + 1) * width] for k in range(3)])
        row = lambda k: jnp.concatenate([v[k] for v in parts], axis=1) if merge > 1 else parts[0][k]
        qb[s], vb[s], ehs_ref[s] = row(0), row(1), row(2)

    lists = seen_lists(steps, tok)
    for qi in range(CORES):
        owner = owners[qi]
        item, rank = ranks_at(len_ref, owner, tok, (tok, LANES), 0)
        lo, hi = item[:, :1] * 16, rank[:, :1]
        for j, b in enumerate(lists[qi]):
            _, e = ranks_at(len_ref, owners[b], tok, (8, tok), 1)
            e = e[:1]
            masks[qi, j] = jnp.where((e >= lo) & (e <= hi), 0.0, -1e30)
    own_item, _ = ranks_at(len_ref, owners[0], tok, (tok, 8), 0)
    picks = (own_item == lax.broadcasted_iota(jnp.int32, (tok, 8), 1)).astype(bf16)

    gwide_ref[0] = (per_token(picks, table(GAMMA_TWO)) * grad_ref[...].astype(f32)).astype(bf16)
    cross = [
        remote(gwide_ref.at[0], gwide_ref.at[1], ms.at[0], mr.at[0], p.twin()),
        remote(theirs, got, ms.at[1], mr.at[1], p.twin()),
        remote(nwide_ref.at[0], nwide_ref.at[1], ms.at[2], mr.at[2], p.twin()),
    ]
    cross[0].start()

    owns[0].wait()
    twins[0].wait()

    def norm_block(b):
        owner = owners[0]
        for i in range(1, blocks):
            owner = jnp.where(b == i, owners[i], owner)
        item, _ = ranks_at(len_ref, owner, tok, (tok, 8), 0)
        pick = (item == lax.broadcasted_iota(jnp.int32, (tok, 8), 1)).astype(bf16)
        normal, _ = norm_parts(win[b].astype(f32))
        scale = per_token(pick, table(SCALE_ONE))
        shift = per_token(pick, table(SHIFT_ONE))
        at = pl.ds(pl.multiple_of(b * tok, tok), tok)
        normed[at, :] = (normal * (1.0 + scale) + shift).astype(bf16)

    def weight(s, k, count=1):
        if merge == 1:
            return wa[s, k * width : (k + count) * width, :]
        rows_of = [
            wa[s * merge + i, (k + j) * width : (k + j + 1) * width, :]
            for j in range(count)
            for i in range(merge)
        ]
        return jnp.concatenate(rows_of, axis=0)

    def keys_block(b):
        at = pl.ds(pl.multiple_of(b * tok, tok), tok)

        def slot(s, _):
            r = dot(normed[at, :], weight(s, 1, 2), 1, 1)
            kv[s, at, :] = r[:, :LANES]
            vv[s, at, :] = (r[:, LANES:] + vb[s]).astype(bf16)
            return 0

        lax.fori_loop(0, pairs, slot, 0)

    @pl.loop(0, CORES)
    def _(b):
        norm_block(b)

    for level in range(bits_of(nd)):
        for step in range(1, nz):
            al.each(step, lambda w, chip: a_spread(w, step, chip).step(level))
    owns[1].wait()
    wout = pltpu.make_async_copy(wa, wa_out, out_sem.at[0])
    wout.start()

    @pl.loop(0, CORES)
    def _(b):
        keys_block(b)
        at = pl.ds(pl.multiple_of(b * tok, tok), tok)

        def slot(s, _):
            qv[s, at, :] = dot(normed[at, :], weight(s, 0), 1, 1) + qb[s]
            return 0

        lax.fori_loop(0, pairs, slot, 0)

    for i in range(rounds):
        any_got = p.core < 0
        for j, go, have, copy in moves:
            if j == i:
                pl.when(have)(copy.wait_recv)
                any_got = any_got | have

        @pl.when(jnp.logical_not(any_got))
        def _():
            win[2 * i + 2] = jnp.zeros((tok, D), bf16)

        twins[i + 1].start()
    for i in range(rounds):
        twins[i + 1].wait()

    @pl.loop(CORES, blocks)
    def _(b):
        norm_block(b)
        keys_block(b)

    outs = [wout]
    for i, (src, dst) in enumerate(((normed, n_out), (qv, q_out), (kv, k_out), (vv, v_out))):
        outs.append(pltpu.make_async_copy(src, dst, out_sem.at[i + 1]))
        outs[-1].start()

    ml.got(1, lambda w, chip: m_spread(w, 1, chip).begin())
    trips = pairs * CORES
    agenda = {}
    for step in range(1, nz):
        at = min(trips - 1, (step * trips) // nz)
        agenda.setdefault(at, []).append(step)

    @pl.loop(0, trips)
    def _(it):
        s, qi = it // CORES, lax.rem(it, CORES)

        @pl.when(qi == 0)
        def _():
            k = kv[s]
            ku[...] = (k * lax.rsqrt(half_sums(k * k) + epsilon)).astype(bf16)
            v = vv[s]
            low = half_lanes(v.shape[0])
            one = jnp.ones_like(v)
            v0[...] = jnp.where(low, v, one)
            v1[...] = jnp.where(low, one, v)

        at = pl.ds(pl.multiple_of(qi * tok, tok), tok)
        q = qv[s, at, :]
        qu = (q * lax.rsqrt(half_sums(q * q) + epsilon) * ehs_ref[s]).astype(bf16)
        qs = [one_half(qu, h) for h in range(2)]
        acc = [None, None]
        for j in range(len(lists[0])):
            b = block_at(lists, qi, j)
            cols = pl.ds(pl.multiple_of(b * tok, tok), tok)
            mask = masks[qi, j]
            for h in range(2):
                w = jnp.exp(dot(qs[h], ku[cols, :], 1, 1) + mask).astype(bf16)
                r = dot(w, (v0 if h == 0 else v1)[cols, :])
                acc[h] = r if acc[h] is None else acc[h] + r
        low = half_lanes(tok)
        other = jnp.where(low, pltpu.roll(acc[0], HEAD, 1), pltpu.roll(acc[1], HEAD, 1))
        o_ref[s, at, :] = (jnp.where(low, acc[0], acc[1]) / other).astype(bf16)
        turned = other.T
        l_ref[s, 0:1, at] = turned[0:1, :]
        l_ref[s, 1:2, at] = turned[HEAD : HEAD + 1, :]

        for when, todo in agenda.items():

            @pl.when(it == when)
            def _():
                for step in todo:
                    if step + 1 < nz:
                        ml.got(step + 1, lambda w, chip: m_spread(w, step + 1, chip).begin())
                    ml.each(step, lambda w, chip: m_spread(w, step, chip).step(0))

    def project(at):
        total = dot(o_ref[0, at, :], weight(0, 3))
        for s in range(1, pairs):
            total += dot(o_ref[s, at, :], weight(s, 3))
        return total

    theirs[...] = project(pl.ds(tok, tok)).astype(bf16)
    cross[1].start()
    first = project(pl.ds(0, tok)) + pb_ref[...]
    cross[1].wait()
    branch = first + got[...].astype(f32)
    branch_ref[...] = branch
    resid = win[0].astype(f32) + per_token(picks, table(GAMMA_ONE)) * branch
    resid_ref[...] = resid
    normal, _ = norm_parts(resid)
    scale = per_token(picks, table(SCALE_TWO))
    shift = per_token(picks, table(SHIFT_TWO))
    nwide_ref[0] = (normal * (1.0 + scale) + shift).astype(bf16)
    cross[2].start()

    for level in range(1, bits_of(nd)):
        for step in range(1, nz):
            ml.each(step, lambda w, chip: m_spread(w, step, chip).step(level))
    cross[0].wait()
    cross[2].wait()
    for step in range(1, nz):
        al.each(step, lambda w, chip: a_spread(w, step, chip).end())
        ml.each(step, lambda w, chip: m_spread(w, step, chip).end())
    al.end()
    ml.end()
    for i, go, have, copy in moves:
        pl.when(go)(copy.wait_send)
    owns[2].wait()
    for c in outs:
        c.wait()


def forward(lengths, tokens, out_grad, part, extra, abias, proj_bias, apack, mpack, steps, nd, width):
    n, _, cols = part.shape
    nz = n // CORES
    tok = tokens.shape[0]
    rounds = len(steps)
    blocks = 2 * rounds + 2
    t, w = CORES * tok, blocks * tok
    pairs = nz * width // LANES
    seen = len(seen_lists(steps, tok)[0])
    dma = pltpu.SemaphoreType.DMA
    vmem = pl.BlockSpec(memory_space=pltpu.VMEM)
    anywhere = pl.BlockSpec(memory_space=pl.ANY)
    out = lambda *shape: jax.ShapeDtypeStruct(shape, f32)
    low = lambda *shape: jax.ShapeDtypeStruct(shape, bf16)
    v = pltpu.VMEM
    return pl.pallas_call(
        functools.partial(forward_body, n, nd, steps, width),
        out_shape=[
            low(w, D),
            out(pairs, t, LANES),
            out(pairs, w, LANES),
            low(pairs, w, LANES),
            low(pairs, t, LANES),
            out(pairs, 8, t),
            low(nz, 4 * width, D),
            low(nz, *mpack.shape),
            out(tok, D),
            out(tok, D),
            low(CORES, tok, D),
            low(CORES, tok, D),
            out(8, 6 * D),
            out(pairs, 1, LANES),
        ],
        in_specs=[pl.BlockSpec(memory_space=pltpu.SMEM), anywhere]
        + [vmem] * 5
        + [anywhere] * 2,
        out_specs=[anywhere] * 4 + [vmem] * 2 + [anywhere] * 2 + [vmem] * 6,
        scratch_shapes=[
            v((blocks, tok, D), bf16),
            v((nz, 4 * width, D), bf16),
            v(part.shape, f32),
            v((n - 1,) + part.shape[1:], f32),
            v((w, D), bf16),
            v((pairs, t, LANES), f32),
            v((pairs, w, LANES), f32),
            v((pairs, w, LANES), bf16),
            v((pairs, 1, LANES), f32),
            v((pairs, 1, LANES), f32),
            v((CORES, seen, tok, tok), f32),
            v((w, LANES), bf16),
            v((w, LANES), bf16),
            v((w, LANES), bf16),
            v((tok, D), bf16),
            v((tok, D), bf16),
            dma((n - 1,)),
            dma((n - 1,)),
            dma((n - 1,)),
            dma((n - 1,)),
            dma((rounds, CORES)),
            dma((rounds, CORES)),
            dma((rounds + 1,)),
            dma((rounds + 1,)),
            dma((2, nz)),
            dma((2, nz)),
            dma((2, nz)),
            dma((2, nz)),
            dma((3,)),
            dma((5,)),
            dma((2, nz, 2, nd)),
            dma((2, nz, 2, nd)),
            dma((2, nz, 2, nd)),
            dma((2, nz, 2, nd)),
            dma((3,)),
            dma((3,)),
        ],
        compiler_params=pltpu.CompilerParams(
            collective_id=0, has_side_effects=True, vmem_limit_bytes=VMEM_LIMIT
        ),
        name="forward",
    )(lengths, tokens, out_grad, part, extra, abias, proj_bias, apack, mpack)


def turn_body(
    n, nd, gx_ref, mlp_ref, resid_ref, branch_ref, g_ref, seg_ref, mod_ref, db_ref, w_ref, gw_ref,
    mid_ref, wide_ref, hg_ref, out_ref, items_ref, sums_ref, theirs, got, send, recv,
):
    p = Place(n, nd)
    tok = g_ref.shape[0]
    greet([p.twin()])
    theirs[0] = gx_ref[pl.ds(tok, tok), :].astype(bf16)
    theirs[1] = mlp_ref[pl.ds(tok, tok), :].astype(bf16)
    copies = [remote(theirs.at[i], got.at[i], send.at[i], recv.at[i], p.twin()) for i in range(2)]
    for c in copies:
        c.start()
    picks = picks_of(seg_ref[...])
    normal, rstd = norm_parts(resid_ref[...])
    scale = per_token(picks, mod_ref[SCALE_TWO])
    grad_final = g_ref[...].astype(f32)
    copies[0].wait()
    second = gx_ref[pl.ds(0, tok), :] + got[0].astype(f32)
    mid = grad_final + norm_back(normal, rstd, second * (1.0 + scale))
    mid_ref[...] = mid
    attn = (per_token(picks, mod_ref[GAMMA_ONE]) * mid).astype(bf16)
    wide_ref[0] = attn
    copies.append(remote(wide_ref.at[0], wide_ref.at[1], send.at[2], recv.at[2], p.twin()))
    copies[2].start()
    copies[1].wait()
    branch = mlp_ref[pl.ds(0, tok), :] + got[1].astype(f32) + db_ref[...]
    gamma = per_token(picks, mod_ref[GAMMA_TWO])
    out_ref[...] = (resid_ref[...] + gamma * branch).astype(bf16)
    items_ref[0] = per_item(picks, mid * branch_ref[...])
    items_ref[1] = per_item(picks, grad_final * branch)
    items_ref[2] = per_item(picks, second * normal)
    items_ref[3] = per_item(picks, second)
    sums_ref[...] = jnp.zeros_like(sums_ref)
    sums_ref[0:1, :] = jnp.sum(attn.astype(f32), axis=0, keepdims=True)
    sums_ref[1:2, :] = jnp.sum(gw_ref[0].astype(f32), axis=0, keepdims=True)
    copies[2].wait()
    for s in range(w_ref.shape[0]):
        for c in range(CORES):
            hg_ref[s, pl.ds(c * tok, tok), :] = dot(
                wide_ref[c], w_ref[s, 3 * LANES :, :], 1, 1
            ).astype(bf16)


def turn(gx, mlp_part, resid, branch, out_grad, seg, mod, down_bias, weights, gwide, n, nd):
    tok = out_grad.shape[0]
    pairs = weights.shape[0]
    dma = pltpu.SemaphoreType.DMA
    vmem = pl.BlockSpec(memory_space=pltpu.VMEM)
    return pl.pallas_call(
        functools.partial(turn_body, n, nd),
        out_shape=[
            jax.ShapeDtypeStruct((tok, D), f32),
            jax.ShapeDtypeStruct((CORES, tok, D), bf16),
            jax.ShapeDtypeStruct((pairs, CORES * tok, LANES), bf16),
            jax.ShapeDtypeStruct((tok, D), bf16),
            jax.ShapeDtypeStruct((4, 8, D), f32),
            jax.ShapeDtypeStruct((8, D), f32),
        ],
        in_specs=[vmem] * 10,
        out_specs=[vmem] * 6,
        scratch_shapes=[
            pltpu.VMEM((2, tok, D), bf16),
            pltpu.VMEM((2, tok, D), bf16),
            dma((3,)),
            dma((3,)),
        ],
        compiler_params=pltpu.CompilerParams(
            collective_id=2, has_side_effects=True, vmem_limit_bytes=48 << 20
        ),
        name="turn",
    )(gx, mlp_part, resid, branch, out_grad, seg, mod, down_bias, weights, gwide)


def mlp_body(x_ref, g_ref, w_ref, bias_ref, mlp_ref, gx_ref, dw_ref, dbias_ref):
    x, g = x_ref[...], g_ref[...]
    units = w_ref.shape[2] * w_ref.shape[3]
    up = w_ref[0, 0].reshape(units, D)
    down = w_ref[0, 1].reshape(units, D)
    pre = dot(x, up, 1, 1) + bias_ref[0]
    square = pre * pre
    th = jnp.tanh(0.7978845608028654 * pre * (1.0 + 0.044715 * square))
    half = 0.5 * (1.0 + th)
    hidden = (pre * half).astype(bf16)
    slope = half + 0.5 * pre * (1.0 - th * th) * (
        0.7978845608028654 * (1.0 + 3.0 * 0.044715 * square)
    )
    gp = (dot(g, down, 1, 1) * slope).astype(bf16)

    @pl.when(pl.program_id(0) == 0)
    def _():
        mlp_ref[...] = jnp.zeros_like(mlp_ref)
        gx_ref[...] = jnp.zeros_like(gx_ref)

    mlp_ref[...] += dot(hidden, down)
    gx_ref[...] += dot(gp, up)
    dw_ref[0, 0] = dot(gp, x, 0, 0).astype(bf16).reshape(dw_ref.shape[2:])
    dw_ref[0, 1] = dot(hidden, g, 0, 0).astype(bf16).reshape(dw_ref.shape[2:])
    dbias_ref[0] = jnp.sum(gp.astype(f32), axis=0, keepdims=True)


def mlp(x, g, weights, bias):
    t = x.shape[0]
    nz, _, nd, piece, _ = weights.shape
    count = min(nd, max(1, 256 // piece))
    per = nd // count
    steps, units = nz * per, count * piece
    whole = lambda *shape: pl.BlockSpec(shape, lambda i: (0,) * len(shape))
    block = pl.BlockSpec((1, 2, count, piece, D), lambda i: (i // per, 0, i % per, 0, 0))
    row = pl.BlockSpec((1, 1, units), lambda i: (i, 0, 0))
    return pl.pallas_call(
        mlp_body,
        grid=(steps,),
        in_specs=[whole(t, D), whole(t, D), block, row],
        out_specs=[whole(t, D), whole(t, D), block, row],
        out_shape=[
            jax.ShapeDtypeStruct((t, D), f32),
            jax.ShapeDtypeStruct((t, D), f32),
            jax.ShapeDtypeStruct(weights.shape, bf16),
            jax.ShapeDtypeStruct((steps, 1, units), f32),
        ],
        compiler_params=pltpu.CompilerParams(vmem_limit_bytes=VMEM_LIMIT),
        name="mlp",
    )(x, g, weights, bias.reshape(steps, 1, units))


class Reduce:
    def __init__(self, place, first, stage, zstage, out, sems):
        self.p, self.first, self.stage, self.zstage, self.out = place, first, stage, zstage, out
        self.ps, self.pr, self.zs, self.zr, self.os, self.or_ = sems
        self.copies, self.all = {}, []

    def held(self, part, level):
        rels = list(range(self.p.nd))
        for bit in self.p.orders[part][:level]:
            rels = [r for r in rels if not (r >> bit) & 1]
        return rels

    def current(self, part, level, chip, rel):
        if level == 0:
            return self.first(part, chip, self.p.dp ^ rel)
        return self.stage(part, level - 1, chip, self.held(part, level).index(rel))

    def send_plane(self, level, o):
        p = self.p
        chip = p.chip(o)
        for part, order in enumerate(p.orders):
            bit = order[level]
            for rel in self.held(part, level):
                if (rel >> bit) & 1:
                    slot = self.held(part, level + 1).index(rel ^ (1 << bit))
                    c = remote(
                        self.current(part, level, chip, rel),
                        self.stage(part, level, chip, slot),
                        self.ps.at[part, level, o, slot],
                        self.pr.at[part, level, o, slot],
                        p.flip(bit),
                    )
                    c.start()
                    self.copies[part, level, o, slot] = c
                    self.all.append(c)

    def add_plane(self, level, o):
        p = self.p
        chip = p.chip(o)
        for part in range(2):
            for slot, rel in enumerate(self.held(part, level + 1)):
                self.copies[part, level, o, slot].wait_recv()
                room = self.stage(part, level, chip, slot)
                mine = self.current(part, level, chip, rel)
                room[...] = (room[...].astype(f32) + mine[...].astype(f32)).astype(bf16)

    def send_line(self, o):
        p = self.p
        m = bits_of(p.nd)
        for part in range(2):
            c = remote(
                self.stage(part, m - 1, p.chip(o), 0),
                self.zstage(part, o),
                self.zs.at[part, o],
                self.zr.at[part, o],
                p.on_chip(o),
            )
            c.start()
            self.copies["z", part, o] = c
            self.all.append(c)

    def end_line(self):
        p = self.p
        m = bits_of(p.nd)
        for part in range(2):
            total = self.stage(part, m - 1, p.z, 0)[...].astype(f32)
            for o in p.far:
                self.copies["z", part, o].wait_recv()
                total = total + self.zstage(part, o)[...].astype(f32)
            self.out(part, p.dp)[...] = total.astype(bf16)
        self.back = Spread(p, self.out, self.os, self.or_)
        self.back.begin()

    def end(self):
        for c in self.all:
            c.wait_send()
        self.back.end()


def finish_body(
    n, nd, steps, dm_ref, da_ref, gn_ref, x_ref, mid_ref, seg_ref, mod_ref, part_ref, extra_ref,
    ym_ref, ya_ref, tg_ref, small_ref,
    mstage, astage, mz, az, gswap, gmine, ghalo, part, held,
    mps, mpr, mzs, mzr, mos, mor, aps, apr, azs, azr, aos, aor,
    gs, gr, hs, hr, s1, r1, s2, r2, s3, r3, s4, r4,
):
    p = Place(n, nd)
    nz, tok = p.nz, x_ref.shape[0]
    rounds = len(steps)
    half = D // 2
    m = bits_of(nd)
    p.greet_all()

    def room(buffer, narrow):
        def at(p_, level, chip, slot):
            base = sum(nd >> (i + 1) for i in range(level))
            return buffer.at[p_, base + slot, chip]

        return at

    cut = lambda part_: pl.ds(part_ * half, half)
    rm = Reduce(
        p,
        lambda q, chip, d: dm_ref.at[chip, q, d],
        room(mstage, False),
        lambda q, o: mz.at[q, o],
        lambda q, d: ym_ref.at[q, d],
        (mps, mpr, mzs, mzr, mos, mor),
    )
    ra = Reduce(
        p,
        lambda q, chip, d: da_ref.at[chip, d, :, cut(q)],
        room(astage, True),
        lambda q, o: az.at[q, o],
        lambda q, d: ya_ref.at[d, :, cut(q)],
        (aps, apr, azs, azr, aos, aor),
    )
    far = p.far + [0]
    gcopies = []
    for i in range(rounds + 1):
        gswap[i] = gn_ref[i, 1].astype(bf16)
        c = remote(gswap.at[i], gmine.at[i], gs.at[i], gr.at[i], p.twin())
        c.start()
        gcopies.append(c)
    for o in far:
        rm.send_plane(0, o)
    moves = []
    for i, per_core in enumerate(steps):
        gcopies[i + 1].wait()
        gmine[i + 1] = (gn_ref[i + 1, 0] + gmine[i + 1].astype(f32)).astype(bf16)
        for c, step in enumerate(per_core):
            if step is None:
                continue
            go = (p.core == c) & (p.z - step >= 0) & (p.z - step < nz)
            got = (p.core == c) & (p.z + step >= 0) & (p.z + step < nz)
            copy = remote(gmine.at[i + 1], ghalo.at[i], hs.at[i, c], hr.at[i, c], p.on_chip(-step))
            pl.when(go)(copy.start)
            moves.append((i, go, got, copy))
    gcopies[0].wait()
    first = gn_ref[0, 0] + gmine[0].astype(f32)
    tg_ref[...] = first
    for i, go, got, copy in moves:

        @pl.when(got)
        def _():
            copy.wait_recv()
            tg_ref[...] += ghalo[i].astype(f32)

    first = tg_ref[...]
    picks = picks_of(seg_ref[...])
    normal, rstd = norm_parts(x_ref[...].astype(f32))
    scale = per_token(picks, mod_ref[SCALE_ONE])
    tg_ref[...] = mid_ref[...] + norm_back(normal, rstd, first * (1.0 + scale))
    part[...] = part_ref[...]
    chunk = 6 * D // n
    for which, values in ((SCALE_ONE, first * normal), (SHIFT_ONE, first)):
        items = per_item(picks, values)
        begin, end = which * D, (which + 1) * D
        for j in range(n):
            a, b = max(begin, j * chunk), min(end, (j + 1) * chunk)
            if a < b:
                part[j, :, a - j * chunk : b - j * chunk] += items[:, a - begin : b - begin]
    line = p.line()
    sums = [remote(part.at[q[1]], held.at[o], s1.at[o], r1.at[o], q) for o, q in enumerate(line)]
    for c in sums:
        c.start()

    def advance(r, level):
        for o in far:
            r.add_plane(level, o)
            if level + 1 < m:
                r.send_plane(level + 1, o)
            elif o:
                r.send_line(o)

    advance(rm, 0)
    for o in far:
        ra.send_plane(0, o)
    for c in sums:
        c.wait()
    total = part[p.me] + extra_ref[...]
    for o in range(n - 1):
        total = total + held[o]
    small_ref[p.core, p.z, p.dp] = total
    mine = small_ref.at[p.core, p.z, p.dp]
    plane = [(lax.rem(p.dp + o, nd), p.me) for o in range(1, nd)]
    sums = [remote(mine, mine, s2.at[o], r2.at[o], q) for o, q in enumerate(plane)]
    for c in sums:
        c.start()
    for level in range(1, m):
        advance(rm, level)
    for c in sums:
        c.wait()
    mine = small_ref.at[p.core, p.z]
    sums = [remote(mine, mine, s3.at[o], r3.at[o], p.on_chip(o)) for o in p.far]
    for c in sums:
        c.start()
    advance(ra, 0)
    rm.end_line()
    for level in range(1, m):
        advance(ra, level)
    for c in sums:
        c.wait()
    mine = small_ref.at[p.core]
    last = remote(mine, mine, s4, r4, p.twin())
    last.start()
    ra.end_line()
    for level in range(m):
        rm.back.step(level)
        ra.back.step(level)
    last.wait()
    rm.end()
    ra.end()
    for i, go, got, copy in moves:
        pl.when(go)(copy.wait_send)


def finish(dm, da, gn, tokens, mid, seg, mod, part, extra, steps, nd):
    n, rows, cols = part.shape
    nz = n // CORES
    tok = tokens.shape[0]
    rounds = len(steps)
    piece, arows = dm.shape[3], da.shape[2]
    dma = pltpu.SemaphoreType.DMA
    vmem = pl.BlockSpec(memory_space=pltpu.VMEM)
    m = bits_of(nd)
    levels = max(1, nd // 2)
    plane = (2, m, nz, levels)
    wide = lambda: [
        dma(plane),
        dma(plane),
        dma((2, nz)),
        dma((2, nz)),
        dma((2, nd)),
        dma((2, nd)),
    ]
    return pl.pallas_call(
        functools.partial(finish_body, n, nd, steps),
        out_shape=[
            jax.ShapeDtypeStruct(dm.shape[1:], bf16),
            jax.ShapeDtypeStruct(da.shape[1:], bf16),
            jax.ShapeDtypeStruct((tok, D), f32),
            jax.ShapeDtypeStruct((CORES, nz, nd, rows, cols), f32),
        ],
        in_specs=[vmem] * 9,
        out_specs=[vmem] * 4,
        scratch_shapes=[
            pltpu.VMEM((2, nd - 1, nz, piece, D), bf16),
            pltpu.VMEM((2, nd - 1, nz, arows, D // 2), bf16),
            pltpu.VMEM((2, nz, piece, D), bf16),
            pltpu.VMEM((2, nz, arows, D // 2), bf16),
            pltpu.VMEM((rounds + 1, tok, D), bf16),
            pltpu.VMEM((rounds + 1, tok, D), bf16),
            pltpu.VMEM((rounds, tok, D), bf16),
            pltpu.VMEM((n, rows, cols), f32),
            pltpu.VMEM((n - 1, rows, cols), f32),
        ]
        + wide()
        + wide()
        + [
            dma((rounds + 1,)),
            dma((rounds + 1,)),
            dma((rounds, CORES)),
            dma((rounds, CORES)),
            dma((n - 1,)),
            dma((n - 1,)),
            dma((nd - 1,)),
            dma((nd - 1,)),
            dma((nz,)),
            dma((nz,)),
            dma,
            dma,
        ],
        compiler_params=pltpu.CompilerParams(
            collective_id=3, has_side_effects=True, vmem_limit_bytes=VMEM_LIMIT
        ),
        name="finish",
    )(dm, da, gn, tokens, mid, seg, mod, part, extra)


def local(
    nd,
    nt,
    tokens,
    class_embed,
    item_lengths,
    token_codes,
    ada_weight,
    ada_bias,
    qkv_weight,
    query_bias,
    value_bias,
    head_scale,
    proj_weight,
    proj_bias,
    up_weight,
    up_bias,
    down_weight,
    down_bias,
    out_grad,
):
    d, t = lax.axis_index("dp"), lax.axis_index("tensor")
    nz = nt // CORES
    z, core = t // CORES, t % CORES
    tok = tokens.shape[0]
    heads = head_scale.shape[0]
    width = heads * HEAD
    wide = nz * width
    pairs = wide // LANES
    units = up_weight.shape[1]
    feat = class_embed.shape[2]

    per_chip = CORES * tok
    seen = [[], []]
    for c in range(CORES):
        for step in range(1, nz):
            if step * per_chip - c * tok - tok < BEHIND:
                seen[c].append(step)
        for step in range(1, nz):
            if (step - 1) * per_chip + c * tok < AHEAD:
                seen[c].append(-step)
    rounds = max(len(s) for s in seen)
    steps = [
        tuple(s[len(s) - 1 - i] if i < len(s) else None for s in seen) for i in range(rounds)
    ]

    chunk = ada_weight.shape[1] // nt
    cond_act = jax.nn.silu(class_embed[0]).astype(bf16)
    ada_part = jnp.dot(cond_act, ada_weight, preferred_element_type=f32)
    part = jnp.pad(ada_part.reshape(SEGS, nt, chunk).transpose(1, 0, 2), ((0, 0), (0, 2), (0, 0)))
    bias_row = jnp.concatenate(
        [
            query_bias,
            value_bias,
            jnp.broadcast_to(jnp.exp(head_scale)[:, None], (heads, HEAD)).reshape(width),
            jnp.zeros((chunk - 3 * width,), f32),
        ]
    )
    extra = jnp.pad(bias_row[None], ((SEGS, 7 - SEGS), (0, 0)))
    abias = jnp.pad(
        jnp.broadcast_to(ada_bias.reshape(nt, 1, chunk), (nt, SEGS, chunk)),
        ((0, 0), (0, 8 - SEGS), (0, 0)),
    )
    apack = jnp.concatenate(
        [qkv_weight.transpose(1, 2, 0).reshape(3 * width, D), proj_weight], axis=0
    )
    mpack = jnp.stack([up_weight.T, down_weight]).reshape(2, nd, units // nd, D)
    (
        normed, q_raw, k_raw, v_in, heads_out, weight_sums, wattn, wmlp, branch, resid, nwide,
        gwide, mod_wide, ehs,
    ) = forward(
        item_lengths[0], tokens, out_grad, part, extra, abias, proj_bias[None], apack, mpack,
        steps, nd, width,
    )
    mod = mod_wide.reshape(8, 6, D).transpose(1, 0, 2)

    segment, scale_ids = item_layout(item_lengths[0])
    rank = segment * 16 + scale_ids
    owners = []
    for s in [(0, 0)] + steps:
        for flip in range(CORES):
            c = core ^ flip
            step = jnp.where(c == 0, nz if s[0] is None else s[0], nz if s[1] is None else s[1])
            chip = z - step
            owners.append(jnp.where((chip >= 0) & (chip < nz), chip * CORES + c, -1))
    blocks = len(owners)
    seg_blocks, rank_blocks = segment.reshape(nt, tok), rank.reshape(nt, tok)
    take = lambda a, o: lax.dynamic_index_in_dim(a, jnp.maximum(o, 0), 0, keepdims=False)
    seg_win = jnp.concatenate([take(seg_blocks, o) for o in owners])
    e_win = jnp.concatenate([jnp.where(o >= 0, take(rank_blocks, o), -1) for o in owners])
    lo = seg_win[: CORES * tok] * 16
    hi = e_win[: CORES * tok]
    e_blocks = e_win.reshape(blocks, tok)
    e_max, e_min = jnp.max(e_blocks, axis=1), jnp.min(e_blocks, axis=1)
    need = (
        (e_max[None, :] >= jnp.min(lo.reshape(CORES, tok), axis=1)[:, None])
        & (e_min[None, :] <= jnp.max(hi.reshape(CORES, tok), axis=1)[:, None])
        & (e_max[None, :] >= 0)
    ).astype(jnp.int32).reshape(CORES * blocks)
    seg_own = seg_win[:tok, None]

    merge = nz // pairs
    weights = (
        wattn.reshape(pairs, merge, 4, width, D)
        .transpose(0, 2, 1, 3, 4)
        .reshape(pairs, 4 * LANES, D)
    )

    up_own = lax.dynamic_index_in_dim(
        up_bias.reshape(nz, CORES, units), core, 1, keepdims=False
    )
    mlp_part, gx_part, dmlp, dbias = mlp(
        nwide.reshape(CORES * tok, D), gwide.reshape(CORES * tok, D), wmlp, up_own
    )
    mid, awide, heads_grad, layer_out, items, sums = turn(
        gx_part, mlp_part, resid, branch, out_grad, seg_own, mod, down_bias[None], weights,
        gwide, nt, nd,
    )
    dattn, gn, head_sums = attend_back(
        need, q_raw, k_raw, v_in, heads_grad, heads_out, weight_sums, ehs, lo[None, :],
        hi[None, :], e_win[:, None], normed, awide.reshape(CORES * tok, D), weights, tok,
    )

    low_codes = 64
    hot = lambda v, k: (v[:, None] == jnp.arange(k, dtype=jnp.int32)[None, :]).astype(bf16)
    hist = dot(
        hot(token_codes // low_codes, NBINS // low_codes),
        hot(token_codes % low_codes, low_codes),
        0,
        0,
    ).reshape(NBINS)
    row_six = jnp.concatenate([sums[0], sums[1], hist])
    to_all = lambda v: jnp.where(
        (jnp.arange(CORES) == core)[None, :, None], v[:, None, :], 0.0
    ).reshape(-1)
    row_seven = jnp.concatenate(
        [
            to_all(dbias.reshape(nz, units)),
            to_all(head_sums[:, 0].reshape(nz, width)),
            to_all(head_sums[:, 1].reshape(nz, width)),
        ]
    )
    hs_part = to_all(jnp.sum(head_sums[:, 2].reshape(nz, heads, HEAD), axis=2)).reshape(nt, heads)
    none = jnp.zeros((SEGS, D), f32)
    mod_part = jnp.concatenate(
        [items[0, :SEGS], items[1, :SEGS], none, items[2, :SEGS], none, items[3, :SEGS]], axis=1
    )
    payload = jnp.concatenate([mod_part, row_six[None], row_seven[None]], axis=0)
    payload = payload.reshape(8, nt, chunk).transpose(1, 0, 2)
    tail = jnp.pad(hs_part[:, None, :], ((0, 0), (7, 0), (0, LANES - heads)))
    own_tail = jnp.pad(
        cond_act.astype(f32), ((0, 8 - SEGS), (chunk, LANES - feat))
    )
    dattn = (
        dattn.reshape(pairs, 4, merge, width, D)
        .transpose(0, 2, 1, 3, 4)
        .reshape(nz, nd, 4 * width // nd, D)
    )
    ymlp, yattn, tokens_grad, small = finish(
        dmlp,
        dattn,
        gn.reshape(rounds + 1, CORES, tok, D),
        tokens,
        mid,
        seg_own,
        mod,
        jnp.concatenate([payload, tail], axis=2),
        own_tail,
        steps,
        nd,
    )

    rows_all = small[..., :chunk].transpose(2, 3, 1, 0, 4).reshape(nd, 8, 6 * D)
    mod_all = rows_all[:, :SEGS].reshape(nd * SEGS, 6 * D)
    mod_own = lax.dynamic_index_in_dim(rows_all, d, 0, keepdims=False)[:SEGS]
    bias_sums = jnp.sum(rows_all[:, SEGS:], axis=0)
    own_small = lax.dynamic_index_in_dim(small, core, 0, keepdims=False)
    own_small = lax.dynamic_index_in_dim(own_small, z, 0, keepdims=False)
    cond_all = own_small[:, :SEGS, chunk : chunk + feat].reshape(nd * SEGS, feat)
    hscale_grad = jnp.sum(own_small[:, 7, chunk : chunk + heads], axis=0)
    adaw_grad = dot(cond_all, mod_all, 0, 0, highest)
    adab_grad = jnp.sum(mod_all, axis=0)
    cond_grad = dot(mod_own, ada_weight.astype(f32), 1, 1, highest)
    embed_grad = jax.vjp(jax.nn.silu, class_embed)[1](cond_grad[None])[0]
    projb_grad, downb_grad = bias_sums[0, :D], bias_sums[0, D : 2 * D]
    code_hist = bias_sums[0, 2 * D :]
    at = lambda base, k: lax.dynamic_slice_in_dim(bias_sums[1], base + t * k, k, 0)
    upb_grad = at(0, units)
    qbias_grad = at(nt * units, width)
    vbias_grad = at(nt * (units + width), width)
    yattn = yattn.reshape(4 * width, D)
    qkvw_grad = yattn[: 3 * width].astype(f32).reshape(3, width, D).transpose(2, 0, 1)
    projw_grad = yattn[3 * width :].astype(f32)
    upw_grad = ymlp[0].reshape(units, D).astype(f32).T
    downw_grad = ymlp[1].reshape(units, D).astype(f32)
    return (
        layer_out,
        tokens_grad,
        embed_grad,
        adaw_grad,
        adab_grad,
        qkvw_grad,
        qbias_grad,
        vbias_grad,
        hscale_grad,
        projw_grad,
        projb_grad,
        upw_grad,
        upb_grad,
        downw_grad,
        downb_grad,
        code_hist,
    )


def solution(mesh):
    placed = (
        P(("dp", "tensor"), None),
        P("dp", None, "tensor"),
        P("dp", None),
        P(("dp", "tensor")),
        P("tensor", None),
        P(),
        P(None, None, "tensor"),
        P("tensor"),
        P("tensor"),
        P("tensor"),
        P("tensor", None),
        P(),
        P(None, "tensor"),
        P(),
        P("tensor", None),
        P(),
        P(("dp", "tensor"), None),
    )
    return jax.shard_map(
        functools.partial(local, mesh.shape["dp"], mesh.shape["tensor"]),
        mesh=mesh,
        in_specs=placed,
        out_specs=(
            P(("dp", "tensor"), None),
            P(("dp", "tensor"), None),
            P("dp", None, "tensor"),
            P("tensor", None),
            P(),
            P(None, None, "tensor"),
            P("tensor"),
            P("tensor"),
            P("tensor"),
            P("tensor", None),
            P(),
            P(None, "tensor"),
            P("tensor"),
            P("tensor", None),
            P(),
            P(),
        ),
        check_vma=False,
    )
```

profile of v0, /device:TPU:0, one launch (start us, length us, event | category | flops | bytes accessed | tf_op | source)
XLA Modules:
  0.0 434.5 jit_solution(17443503346583391252)
XLA Ops:
  2.0 1.5 copy.76
  3.5 2.9 pad_maximum_fusion.mpack_ref
  6.4 1.6 copy.87
  7.9 2.0 convolution_bitcast_fusion.1
  10.9 1.0 pad_maximum_fusion.1.apack_ref
  13.5 128.2 %forward.1 = (bf16[1536,1024]{1,0:T(8,128)(2,1)}, f32[4,512,128]{2,1,0:T(8,128)}, f32[4,1536,128]{2,1,0:T(8,128)}, bf16[4,1536,128]{2,1,0:T(8,128)(2,1)}, bf16[4...) custom-call(s32[6]{0:T(128)} %bitcast.164, ...), custom_call_target="tpu_custom_call" | custom-call | tf_op jit(solution)/shard_map/forward/pallas_call | solution.py:750
  141.7 22.4 %mlp.1 = (f32[512,1024]{1,0:T(8,128)}, f32[512,1024]{1,0:T(8,128)}, bf16[4,2,4,128,1024]{4,3,2,1,0:T(8,128)(2,1)}, f32[8,1,256]{2,1,0:T(1,128)}) custom-call(bf16[512,1024]{1,0:T(8,128)(2,1)} %bitcast.131, bf16[512,1024]{1,0:T(8,128)(2,1)} %bitcast.128, bf16[4,2,4,128,1024]{4,3,2,1,0:T(8,128)(2,1)} %get-tuple-element.49.w_ref, f32[8,1,256]{2,1,0:T(1,128)} %bitcast.139), custom_call_target="tpu_custom_call" | custom-call | tf_op jit(solution)/shard_map/mlp/pallas_call | solution.py:926
  164.6 9.6 %turn.1 = (f32[256,1024]{1,0:T(8,128)S(1)}, bf16[2,256,1024]{2,1,0:T(8,128)(2,1)S(1)}, bf16[4,512,128]{2,1,0:T(8,128)(2,1)S(1)}, bf16[256,1024]{1,0:T(8,128)(2,1...) custom-call(f32[512,1024]{1,0:T(8,128)} %get-tuple-element.50.gx_ref, f32[512,1024]{1,0:T(8,128)} %get-tuple-element.51.mlp_ref, ...), custom_call_target="tpu_custom_call" | custom-call | tf_op jit(solution)/shard_map/turn/pallas_call | solution.py:865
  174.2 1.0 copy-done.2
  175.2 1.0 copy-done.3
  178.8 1.1 broadcast_in_dim.201.e_ref
  180.6 39.9 %attend_back.1 = (bf16[4,512,1024]{2,1,0:T(8,128)(2,1)}, f32[1536,1024]{1,0:T(8,128)}, f32[4,8,128]{2,1,0:T(8,128)}) custom-call(s32[12]{0:T(128)} %reshape.266.need_ref, f32[4,512,128]{2,1,0:T(8,128)} %get-tuple-element.58.q_ref, f32[4,1536,128]{2,1,0:T(8,128)} %get-tuple-element.59.k_ref, bf16[4,1536,128]{2,1,0:T(8,128)(2,1)} %get-tuple-element.60.v_ref, ...), custom_call_target="tpu_custom_call" | custom-call | tf_op jit(solution)/shard_map/attend_back/pallas_call | solution.py:343
  223.3 183.3 %finish.1 = (bf16[2,4,128,1024]{3,2,1,0:T(8,128)(2,1)}, bf16[4,128,1024]{2,1,0:T(8,128)(2,1)}, f32[256,1024]{1,0:T(8,128)}, f32[2,4,4,8,896]{4,3,2,1,0:T(8,128)}) custom-call(bf16[4,2,4,128,1024]{4,3,2,1,0:T(8,128)(2,1)} %get-tuple-element.57.dm_ref, bf16[4,4,128,1024]{3,2,1,0:T(8,128)(2,1)} %bitcast.127, f32[3,2,256,1024]{3,2,1,0:T(8,128)} %bitcast.125, ...), custom_call_target="tpu_custom_call" | custom-call | tf_op jit(solution)/shard_map/finish/pallas_call | solution.py:1178
  406.6 1.2 slice_bitcast_fusion
  409.0 0.9 dynamic-slice_bitcast_fusion.2
  410.0 4.3 convolution_bitcast_fusion
  414.3 1.1 fusion.25
  415.7 1.8 copy.84
  417.6 2.9 bitcast_convert_fusion
  420.4 1.3 convert_bitcast_fusion
  421.8 3.1 copy.86
  428.1 1.3 fusion.15
  430.0 1.8 bitcast_convert_fusion.2
  433.1 1.0 copy.143
  (130 shorter events, 16.9 us)
Async XLA Ops:
  3.5 2.9 copy-start.8
  6.4 1.6 copy-start.15
  6.4 4.2 copy-start.13
  7.9 3.0 copy-start.14
  9.9 2.1 copy-start.16
  10.6 2.1 copy-start.23
  10.6 2.2 copy-start.21
  10.6 2.2 copy-start.22
  141.7 22.4 %copy-start.20 = (s32[1,6]{1,0:T(1,128)S(1)}, s32[1,6]{1,0:T(1,128)}, u32[]{:S(2)}) copy-start(s32[1,6]{1,0:T(1,128)} %param.19) | copy-start | bytes 76
  141.7 22.9 %copy-start = (bf16[256,1024]{1,0:T(8,128)(2,1)S(1)}, bf16[256,1024]{1,0:T(8,128)(2,1)}, u32[]{:S(2)}) copy-start(bf16[256,1024]{1,0:T(8,128)(2,1)} %g_ref.1) | copy-start | bytes 1572868
  141.7 22.9 %copy-start.4 = (f32[256,1024]{1,0:T(8,128)S(1)}, f32[256,1024]{1,0:T(8,128)}, u32[]{:S(2)}) copy-start(f32[256,1024]{1,0:T(8,128)} %get-tuple-element.52.resid_ref) | copy-start | bytes 3145732
  141.7 22.9 %copy-start.5 = (f32[8,6144]{1,0:T(8,128)S(1)}, f32[8,6144]{1,0:T(8,128)}, u32[]{:S(2)}) copy-start(f32[8,6144]{1,0:T(8,128)} %get-tuple-element.54) | copy-start | bytes 589828
  141.7 22.9 %copy-start.7 = (f32[1024]{0:T(1024)S(1)}, f32[1024]{0:T(1024)}, u32[]{:S(2)}) copy-start(f32[1024]{0:T(1024)} %param.32) | copy-start | bytes 12292
  164.5 9.6 %copy-start.1 = (s32[256,1]{1,0:T(8,128)}, s32[256,1]{1,0:T(8,128)S(1)}, u32[]{:S(2)}) copy-start(s32[256,1]{1,0:T(8,128)S(1)} %copy.77.seg_ref) | copy-start | bytes 3076
  164.6 12.4 %copy-start.19 = (s32[256]{0:T(256)S(1)}, s32[256]{0:T(256)}, u32[]{:S(2)}) copy-start(s32[256]{0:T(256)} %param.20) | copy-start | bytes 3076
  174.2 1.0 copy-start.2
  175.2 1.0 copy-start.3
  176.1 0.8 copy-start.6
  177.9 2.7 copy-start.17
  180.6 40.8 %copy-start.18 = (f32[8,1,256]{2,1,0:T(1,128)S(1)}, f32[8,1,256]{2,1,0:T(1,128)}, u32[]{:S(2)}) copy-start(f32[8,1,256]{2,1,0:T(1,128)} %get-tuple-element.72) | copy-start | bytes 24580
  409.9 4.3 copy-start.10
  417.6 2.9 copy-start.12
  421.8 6.3 %copy-start.9 = (bf16[128,6144]{1,0:T(8,128)(2,1)S(1)}, bf16[128,6144]{1,0:T(8,128)(2,1)}, u32[]{:S(2)}) copy-start(bf16[128,6144]{1,0:T(8,128)(2,1)} %param.21) | copy-start | bytes 4718596
  428.1 5.0 %copy-start.11 = (f32[256,1024]{1,0:T(8,128)S(1)}, f32[256,1024]{1,0:T(8,128)}, u32[]{:S(2)}) copy-start(f32[256,1024]{1,0:T(8,128)} %get-tuple-element.186) | copy-start | bytes 3145732
where the time goes:
time: 438 us; the launch traced here: 435 us
  Pallas kernels  383 us (87%)
  local copies, waits for them, and re-layouts  27 us (6%)
  other arithmetic  14.8 us (3%)
  matrix products  7.88 us (2%)
    pallas_call x1, Pallas kernels, finish(): pl.pallas_call(functools.partial(finish_body, n, nd, steps), out_shape=[j...  183 us
    pallas_call x1, Pallas kernels, forward(): pl.pallas_call(functools.partial(forward_body, n, nd, steps, width), out_...  128 us
    pallas_call x1, Pallas kernels, attend_back(): pl.pallas_call(functools.partial(back_body, block, nq, nk), grid_spec=plt...  39.9 us
    pallas_call x1, Pallas kernels, mlp(): pl.pallas_call(mlp_body, grid=(steps,), in_specs=[whole(t, D), whole(t, D...  22.4 us
    pallas_call x1, Pallas kernels, turn(): pl.pallas_call(functools.partial(turn_body, n, nd), out_shape=[jax.ShapeD...  9.56 us

commit v1 on v0

--- a/solution.py
+++ b/solution.py
@@ -259,129 +259,6 @@
 def one_half(x, h):
     low = half_lanes(x.shape[0])
     return jnp.where(low if h == 0 else jnp.logical_not(low), x, jnp.zeros_like(x))
-
-
-def back_body(
-    block, nq, nk, need_ref, q_ref, k_ref, v_ref, g_ref, o_ref, l_ref, ehs_ref, lo_ref, hi_ref,
-    e_ref, n_ref, a_ref, w_ref, dw_ref, gn_ref, sums_ref, ku, dk, dv, dq, gqs, gkv,
-):
-    t = nq * block
-    k = k_ref[0]
-    rk = lax.rsqrt(half_sums(k * k) + epsilon)
-    ku[...] = (k * rk).astype(bf16)
-    dk[...] = jnp.zeros_like(dk)
-    dv[...] = jnp.zeros_like(dv)
-    ehs = ehs_ref[0]
-    qsum = jnp.zeros((1, LANES), f32)
-    hsum = jnp.zeros((1, LANES), f32)
-    for qi in range(nq):
-        rows = pl.ds(qi * block, block)
-        q = q_ref[0, rows, :]
-        rq = lax.rsqrt(half_sums(q * q) + epsilon)
-        qhat = q * rq
-        qu = (qhat * ehs).astype(bf16)
-        qs = [one_half(qu, h) for h in range(2)]
-        g = g_ref[0, rows, :]
-        gs = [one_half(g, h) for h in range(2)]
-        turned = (g.astype(f32) * o_ref[0, rows, :].astype(f32)).T
-        deltas = [
-            jnp.sum(turned[:HEAD], axis=0, keepdims=True),
-            jnp.sum(turned[HEAD:], axis=0, keepdims=True),
-        ]
-        invs = [1.0 / l_ref[0, h : h + 1, rows] for h in range(2)]
-        lo, hi = lo_ref[:, rows], hi_ref[:, rows]
-        dq[...] = jnp.zeros_like(dq)
-        for ki in range(nk):
-
-            @pl.when(need_ref[qi * nk + ki] > 0)
-            def _():
-                cols = pl.ds(ki * block, block)
-                e = e_ref[cols, :]
-                allowed = (e >= lo) & (e <= hi)
-                kb, vb = ku[cols, :], v_ref[0, cols, :]
-                for h in range(2):
-                    s = dot(kb, qs[h], 1, 1)
-                    p = jnp.where(allowed, jnp.exp(s) * invs[h], 0.0)
-                    dp = dot(vb, gs[h], 1, 1)
-                    ds = (p * (dp - deltas[h])).astype(bf16)
-                    dv[cols, :] += dot(p.astype(bf16), gs[h])
-                    dk[cols, :] += dot(ds, qs[h])
-                    dq[...] += dot(ds, one_half(kb, h), 0, 0)
-
-        d = dq[...]
-        hsum = hsum + jnp.sum(d * qhat * ehs, axis=0, keepdims=True)
-        gq = (ehs * rq * (d - qhat * half_sums(qhat * d))).astype(bf16)
-        gqs[rows, :] = gq
-        qsum = qsum + jnp.sum(gq.astype(f32), axis=0, keepdims=True)
-    khat = k * rk
-    d = dk[...]
-    gkv[:, :LANES] = (rk * (d - khat * half_sums(khat * d))).astype(bf16)
-    gv = dv[...].astype(bf16)
-    gkv[:, LANES:] = gv
-    sums_ref[...] = jnp.zeros_like(sums_ref)
-    sums_ref[0, 0:1, :] = qsum
-    sums_ref[0, 1:2, :] = jnp.sum(gv.astype(f32), axis=0, keepdims=True)
-    sums_ref[0, 2:3, :] = hsum
-    dw_ref[0, :LANES, :] = dot(gqs[...], n_ref[:t, :], 0, 0).astype(bf16)
-    dw_ref[0, LANES : 3 * LANES, :] = dot(gkv[...], n_ref[...], 0, 0).astype(bf16)
-    dw_ref[0, 3 * LANES :, :] = dot(o_ref[0], a_ref[...], 0, 0).astype(bf16)
-
-    @pl.when(pl.program_id(0) == 0)
-    def _():
-        gn_ref[...] = jnp.zeros_like(gn_ref)
-
-    gn_ref[...] += dot(gkv[...], w_ref[0, LANES : 3 * LANES, :])
-    gn_ref[:t, :] += dot(gqs[...], w_ref[0, :LANES, :])
-
-
-def attend_back(need, q, k, v, g, o, l, ehs, lo_row, hi_row, e_col, normed, wide, weights, block):
-    pairs, t, _ = q.shape
-    w = k.shape[1]
-    nq, nk = t // block, w // block
-    slot = lambda rows: pl.BlockSpec((1, rows, LANES), lambda i, *_: (i, 0, 0))
-    whole = lambda *shape: pl.BlockSpec(shape, lambda i, *_: (0,) * len(shape))
-    return pl.pallas_call(
-        functools.partial(back_body, block, nq, nk),
-        grid_spec=pltpu.PrefetchScalarGridSpec(
-            num_scalar_prefetch=1,
-            grid=(pairs,),
-            in_specs=[
-                slot(t),
-                slot(w),
-                slot(w),
-                slot(t),
-                slot(t),
-                pl.BlockSpec((1, 8, t), lambda i, *_: (i, 0, 0)),
-                slot(1),
-                whole(1, t),
-                whole(1, t),
-                whole(w, 1),
-                whole(w, D),
-                whole(t, D),
-                pl.BlockSpec((1, 4 * LANES, D), lambda i, *_: (i, 0, 0)),
-            ],
-            out_specs=[
-                pl.BlockSpec((1, 4 * LANES, D), lambda i, *_: (i, 0, 0)),
-                whole(w, D),
-                slot(8),
-            ],
-            scratch_shapes=[
-                pltpu.VMEM((w, LANES), bf16),
-                pltpu.VMEM((w, LANES), f32),
-                pltpu.VMEM((w, LANES), f32),
-                pltpu.VMEM((block, LANES), f32),
-                pltpu.VMEM((t, LANES), bf16),
-                pltpu.VMEM((w, 2 * LANES), bf16),
-            ],
-        ),
-        out_shape=[
-            jax.ShapeDtypeStruct((pairs, 4 * LANES, D), bf16),
-            jax.ShapeDtypeStruct((w, D), f32),
-            jax.ShapeDtypeStruct((pairs, 8, LANES), f32),
-        ],
-        compiler_params=pltpu.CompilerParams(vmem_limit_bytes=VMEM_LIMIT),
-        name="attend_back",
-    )(need, q, k, v, g, o, l, ehs, lo_row, hi_row, e_col, normed, wide, weights)
 
 
 def ranks_at(lengths_ref, owner, tok, shape, axis):
@@ -814,81 +691,9 @@
     )(lengths, tokens, out_grad, part, extra, abias, proj_bias, apack, mpack)
 
 
-def turn_body(
-    n, nd, gx_ref, mlp_ref, resid_ref, branch_ref, g_ref, seg_ref, mod_ref, db_ref, w_ref, gw_ref,
-    mid_ref, wide_ref, hg_ref, out_ref, items_ref, sums_ref, theirs, got, send, recv,
-):
-    p = Place(n, nd)
-    tok = g_ref.shape[0]
-    greet([p.twin()])
-    theirs[0] = gx_ref[pl.ds(tok, tok), :].astype(bf16)
-    theirs[1] = mlp_ref[pl.ds(tok, tok), :].astype(bf16)
-    copies = [remote(theirs.at[i], got.at[i], send.at[i], recv.at[i], p.twin()) for i in range(2)]
-    for c in copies:
-        c.start()
-    picks = picks_of(seg_ref[...])
-    normal, rstd = norm_parts(resid_ref[...])
-    scale = per_token(picks, mod_ref[SCALE_TWO])
-    grad_final = g_ref[...].astype(f32)
-    copies[0].wait()
-    second = gx_ref[pl.ds(0, tok), :] + got[0].astype(f32)
-    mid = grad_final + norm_back(normal, rstd, second * (1.0 + scale))
-    mid_ref[...] = mid
-    attn = (per_token(picks, mod_ref[GAMMA_ONE]) * mid).astype(bf16)
-    wide_ref[0] = attn
-    copies.append(remote(wide_ref.at[0], wide_ref.at[1], send.at[2], recv.at[2], p.twin()))
-    copies[2].start()
-    copies[1].wait()
-    branch = mlp_ref[pl.ds(0, tok), :] + got[1].astype(f32) + db_ref[...]
-    gamma = per_token(picks, mod_ref[GAMMA_TWO])
-    out_ref[...] = (resid_ref[...] + gamma * branch).astype(bf16)
-    items_ref[0] = per_item(picks, mid * branch_ref[...])
-    items_ref[1] = per_item(picks, grad_final * branch)
-    items_ref[2] = per_item(picks, second * normal)
-    items_ref[3] = per_item(picks, second)
-    sums_ref[...] = jnp.zeros_like(sums_ref)
-    sums_ref[0:1, :] = jnp.sum(attn.astype(f32), axis=0, keepdims=True)
-    sums_ref[1:2, :] = jnp.sum(gw_ref[0].astype(f32), axis=0, keepdims=True)
-    copies[2].wait()
-    for s in range(w_ref.shape[0]):
-        for c in range(CORES):
-            hg_ref[s, pl.ds(c * tok, tok), :] = dot(
-                wide_ref[c], w_ref[s, 3 * LANES :, :], 1, 1
-            ).astype(bf16)
-
-
-def turn(gx, mlp_part, resid, branch, out_grad, seg, mod, down_bias, weights, gwide, n, nd):
-    tok = out_grad.shape[0]
-    pairs = weights.shape[0]
-    dma = pltpu.SemaphoreType.DMA
-    vmem = pl.BlockSpec(memory_space=pltpu.VMEM)
-    return pl.pallas_call(
-        functools.partial(turn_body, n, nd),
-        out_shape=[
-            jax.ShapeDtypeStruct((tok, D), f32),
-            jax.ShapeDtypeStruct((CORES, tok, D), bf16),
-            jax.ShapeDtypeStruct((pairs, CORES * tok, LANES), bf16),
-            jax.ShapeDtypeStruct((tok, D), bf16),
-            jax.ShapeDtypeStruct((4, 8, D), f32),
-            jax.ShapeDtypeStruct((8, D), f32),
-        ],
-        in_specs=[vmem] * 10,
-        out_specs=[vmem] * 6,
-        scratch_shapes=[
-            pltpu.VMEM((2, tok, D), bf16),
-            pltpu.VMEM((2, tok, D), bf16),
-            dma((3,)),
-            dma((3,)),
-        ],
-        compiler_params=pltpu.CompilerParams(
-            collective_id=2, has_side_effects=True, vmem_limit_bytes=48 << 20
-        ),
-        name="turn",
-    )(gx, mlp_part, resid, branch, out_grad, seg, mod, down_bias, weights, gwide)
-
-
-def mlp_body(x_ref, g_ref, w_ref, bias_ref, mlp_ref, gx_ref, dw_ref, dbias_ref):
+def mlp_body(x_ref, g_ref, w_ref, bias_ref, mine_ref, theirs_ref, dw_ref, dbias_ref, mlp, gx):
     x, g = x_ref[...], g_ref[...]
+    tok = mine_ref.shape[1]
     units = w_ref.shape[2] * w_ref.shape[3]
     up = w_ref[0, 0].reshape(units, D)
     down = w_ref[0, 1].reshape(units, D)
@@ -904,18 +709,25 @@
 
     @pl.when(pl.program_id(0) == 0)
     def _():
-        mlp_ref[...] = jnp.zeros_like(mlp_ref)
-        gx_ref[...] = jnp.zeros_like(gx_ref)
-
-    mlp_ref[...] += dot(hidden, down)
-    gx_ref[...] += dot(gp, up)
+        mlp[...] = jnp.zeros_like(mlp)
+        gx[...] = jnp.zeros_like(gx)
+
+    mlp[...] += dot(hidden, down)
+    gx[...] += dot(gp, up)
     dw_ref[0, 0] = dot(gp, x, 0, 0).astype(bf16).reshape(dw_ref.shape[2:])
     dw_ref[0, 1] = dot(hidden, g, 0, 0).astype(bf16).reshape(dw_ref.shape[2:])
     dbias_ref[0] = jnp.sum(gp.astype(f32), axis=0, keepdims=True)
 
+    @pl.when(pl.program_id(0) == pl.num_programs(0) - 1)
+    def _():
+        for i, v in enumerate((gx, mlp)):
+            mine_ref[i] = v[:tok, :]
+            theirs_ref[i] = v[tok:, :].astype(bf16)
+
 
 def mlp(x, g, weights, bias):
     t = x.shape[0]
+    tok = t // CORES
     nz, _, nd, piece, _ = weights.shape
     count = min(nd, max(1, 256 // piece))
     per = nd // count
@@ -927,23 +739,27 @@
         mlp_body,
         grid=(steps,),
         in_specs=[whole(t, D), whole(t, D), block, row],
-        out_specs=[whole(t, D), whole(t, D), block, row],
+        out_specs=[whole(2, tok, D), whole(2, tok, D), block, row],
         out_shape=[
-            jax.ShapeDtypeStruct((t, D), f32),
-            jax.ShapeDtypeStruct((t, D), f32),
+            jax.ShapeDtypeStruct((2, tok, D), f32),
+            jax.ShapeDtypeStruct((2, tok, D), bf16),
             jax.ShapeDtypeStruct(weights.shape, bf16),
             jax.ShapeDtypeStruct((steps, 1, units), f32),
         ],
+        scratch_shapes=[pltpu.VMEM((t, D), f32), pltpu.VMEM((t, D), f32)],
         compiler_params=pltpu.CompilerParams(vmem_limit_bytes=VMEM_LIMIT),
         name="mlp",
     )(x, g, weights, bias.reshape(steps, 1, units))
 
 
 class Reduce:
-    def __init__(self, place, first, stage, zstage, out, sems):
-        self.p, self.first, self.stage, self.zstage, self.out = place, first, stage, zstage, out
-        self.ps, self.pr, self.zs, self.zr, self.os, self.or_ = sems
-        self.copies, self.all = {}, []
+    def __init__(self, place, sent, kept, stage, zstage, final, out, sems):
+        self.p, self.sent, self.kept = place, sent, kept
+        self.stage, self.zstage, self.final = stage, zstage, final
+        self.ps, self.pr, self.zs, self.zr, self.os, self.or_, self.fs = sems
+        self.m = bits_of(place.nd)
+        self.back = Spread(place, out, self.os, self.or_)
+        self.out = out
 
     def held(self, part, level):
         rels = list(range(self.p.nd))
@@ -953,170 +769,421 @@
 
     def current(self, part, level, chip, rel):
         if level == 0:
-            return self.first(part, chip, self.p.dp ^ rel)
+            bit = self.p.orders[part][0]
+            return (self.sent if (rel >> bit) & 1 else self.kept)(part, chip, self.p.dp ^ rel)
         return self.stage(part, level - 1, chip, self.held(part, level).index(rel))
 
-    def send_plane(self, level, o):
-        p = self.p
-        chip = p.chip(o)
-        for part, order in enumerate(p.orders):
+    def plane(self, level, chip):
+        for part, order in enumerate(self.p.orders):
             bit = order[level]
             for rel in self.held(part, level):
                 if (rel >> bit) & 1:
                     slot = self.held(part, level + 1).index(rel ^ (1 << bit))
-                    c = remote(
+                    yield remote(
                         self.current(part, level, chip, rel),
                         self.stage(part, level, chip, slot),
-                        self.ps.at[part, level, o, slot],
-                        self.pr.at[part, level, o, slot],
-                        p.flip(bit),
+                        self.ps.at[part, level, chip, slot],
+                        self.pr.at[part, level, chip, slot],
+                        self.p.flip(bit),
                     )
-                    c.start()
-                    self.copies[part, level, o, slot] = c
-                    self.all.append(c)
-
-    def add_plane(self, level, o):
-        p = self.p
-        chip = p.chip(o)
+
+    def send_plane(self, level, chip):
+        for c in self.plane(level, chip):
+            c.start()
+
+    def add_plane(self, level, chip):
+        for c in self.plane(level, chip):
+            c.wait_recv()
         for part in range(2):
             for slot, rel in enumerate(self.held(part, level + 1)):
-                self.copies[part, level, o, slot].wait_recv()
                 room = self.stage(part, level, chip, slot)
                 mine = self.current(part, level, chip, rel)
                 room[...] = (room[...].astype(f32) + mine[...].astype(f32)).astype(bf16)
 
-    def send_line(self, o):
-        p = self.p
-        m = bits_of(p.nd)
+    def line(self, o):
         for part in range(2):
-            c = remote(
-                self.stage(part, m - 1, p.chip(o), 0),
+            yield part, remote(
+                self.stage(part, self.m - 1, self.p.chip(o), 0),
                 self.zstage(part, o),
                 self.zs.at[part, o],
                 self.zr.at[part, o],
-                p.on_chip(o),
+                self.p.on_chip(o),
             )
-            c.start()
-            self.copies["z", part, o] = c
-            self.all.append(c)
+
+    def advance(self, level, then=None):
+        for o in self.p.far + [0]:
+            self.add_plane(level, self.p.chip(o))
+            if level + 1 < self.m:
+                self.send_plane(level + 1, self.p.chip(o))
+            elif o:
+                for _, c in self.line(o):
+                    c.start()
 
     def end_line(self):
         p = self.p
-        m = bits_of(p.nd)
+        for o in p.far:
+            for _, c in self.line(o):
+                c.wait_recv()
+        puts = []
         for part in range(2):
-            total = self.stage(part, m - 1, p.z, 0)[...].astype(f32)
+            total = self.stage(part, self.m - 1, p.z, 0)[...].astype(f32)
             for o in p.far:
-                self.copies["z", part, o].wait_recv()
                 total = total + self.zstage(part, o)[...].astype(f32)
-            self.out(part, p.dp)[...] = total.astype(bf16)
-        self.back = Spread(p, self.out, self.os, self.or_)
+            self.final(part)[...] = total.astype(bf16)
+            puts.append(
+                pltpu.make_async_copy(self.final(part), self.out(part, p.dp), self.fs.at[part])
+            )
+            puts[-1].start()
+        for c in puts:
+            c.wait()
         self.back.begin()
 
     def end(self):
-        for c in self.all:
-            c.wait_send()
+        for level in range(self.m):
+            for chip in range(self.p.nz):
+                for c in self.plane(level, chip):
+                    c.wait_send()
+        for o in self.p.far:
+            for _, c in self.line(o):
+                c.wait_send()
         self.back.end()
 
 
-def finish_body(
-    n, nd, steps, dm_ref, da_ref, gn_ref, x_ref, mid_ref, seg_ref, mod_ref, part_ref, extra_ref,
-    ym_ref, ya_ref, tg_ref, small_ref,
-    mstage, astage, mz, az, gswap, gmine, ghalo, part, held,
-    mps, mpr, mzs, mzr, mos, mor, aps, apr, azs, azr, aos, aor,
+def backward_body(
+    n, nd, steps, width, len_ref, mine_ref, theirs_ref, x_ref, g_ref, gm_ref, branch_ref, mod_ref,
+    db_ref, dbias_ref, hist_ref, extra_ref, l_ref, ehs_ref, dm_ref, n_hbm, q_hbm, k_hbm, v_hbm,
+    o_hbm, wa_hbm,
+    out_ref, ym_ref, ya_ref, tg_ref, small_ref,
+    got, awide, spare, normed, wp, qs_, ks_, vs_, os_, ku, kut, dk, dv, gqs, gkv, masks,
+    dmk, mstage, mz, mfinal, da, astage, az, afinal, gmine, ghalo, pay, part, held,
+    xs, xr, load, wl, ld, mks,
+    mps, mpr, mzs, mzr, mos, mor, mfs, aps, apr, azs, azr, aos, aor, afs,
     gs, gr, hs, hr, s1, r1, s2, r2, s3, r3, s4, r4,
 ):
     p = Place(n, nd)
     nz, tok = p.nz, x_ref.shape[0]
     rounds = len(steps)
+    blocks = 2 * rounds + 2
+    pairs = l_ref.shape[0]
+    merge = LANES // width
+    arows = 4 * width // nd
+    units = dbias_ref.shape[1]
+    t = CORES * tok
     half = D // 2
     m = bits_of(nd)
-    p.greet_all()
-
-    def room(buffer, narrow):
-        def at(p_, level, chip, slot):
-            base = sum(nd >> (i + 1) for i in range(level))
-            return buffer.at[p_, base + slot, chip]
-
-        return at
-
-    cut = lambda part_: pl.ds(part_ * half, half)
+    chunk = 6 * D // n
+    owners = owners_of(p, steps)
+    table = lambda which: mod_ref[:, which * D : (which + 1) * D]
+
+    def base(level):
+        return sum(nd >> (i + 1) for i in range(level))
+
+    def kept_slot(q, d):
+        bit = p.orders[q][0]
+        return ((d >> (bit + 1)) << bit) | (d & ((1 << bit) - 1))
+
+    cut = lambda q: pl.ds(q * half, half)
     rm = Reduce(
         p,
         lambda q, chip, d: dm_ref.at[chip, q, d],
-        room(mstage, False),
-        lambda q, o: mz.at[q, o],
+        lambda q, chip, d: dmk.at[q, chip, kept_slot(q, d)],
+        lambda q, level, chip, slot: mstage.at[q, base(level) + slot, chip],
+        lambda q, o: mz.at[q, o - 1],
+        lambda q: mfinal.at[q],
         lambda q, d: ym_ref.at[q, d],
-        (mps, mpr, mzs, mzr, mos, mor),
-    )
+        (mps, mpr, mzs, mzr, mos, mor, mfs),
+    )
+    a_own = lambda q, chip, d: da.at[chip, pl.ds(d * arows, arows), cut(q)]
     ra = Reduce(
         p,
-        lambda q, chip, d: da_ref.at[chip, d, :, cut(q)],
-        room(astage, True),
-        lambda q, o: az.at[q, o],
-        lambda q, d: ya_ref.at[d, :, cut(q)],
-        (aps, apr, azs, azr, aos, aor),
-    )
+        a_own,
+        a_own,
+        lambda q, level, chip, slot: astage.at[q, base(level) + slot, chip],
+        lambda q, o: az.at[q, o - 1],
+        lambda q: afinal.at[q],
+        lambda q, d: ya_ref.at[pl.ds(d * arows, arows), cut(q)],
+        (aps, apr, azs, azr, aos, aor, afs),
+    )
+    p.greet_all()
     far = p.far + [0]
-    gcopies = []
-    for i in range(rounds + 1):
-        gswap[i] = gn_ref[i, 1].astype(bf16)
-        c = remote(gswap.at[i], gmine.at[i], gs.at[i], gr.at[i], p.twin())
+    swaps = [remote(theirs_ref.at[i], got.at[i], xs.at[i], xr.at[i], p.twin()) for i in range(2)]
+    swaps.append(remote(awide.at[0], awide.at[1], xs.at[2], xr.at[2], p.twin()))
+    swaps[0].start()
+    swaps[1].start()
+    for o in far:
+        rm.send_plane(0, p.chip(o))
+    loads = [
+        pltpu.make_async_copy(wa_hbm.at[:, pl.ds(3 * width, width)], wp, load.at[0]),
+        pltpu.make_async_copy(n_hbm, normed.at[pl.ds(0, blocks * tok)], load.at[1]),
+    ]
+    for c in loads:
         c.start()
-        gcopies.append(c)
-    for o in far:
-        rm.send_plane(0, o)
+
+    def fetch(s, slot):
+        return [
+            pltpu.make_async_copy(src.at[s], dst.at[slot], ld.at[i, slot])
+            for i, (src, dst) in enumerate(
+                ((q_hbm, qs_), (k_hbm, ks_), (v_hbm, vs_), (o_hbm, os_))
+            )
+        ]
+
+    for c in fetch(0, 0):
+        c.start()
+    keeps = []
+    for q in range(2):
+        for rel in rm.held(q, 1):
+            d = p.dp ^ rel
+            keeps.append(
+                pltpu.make_async_copy(
+                    dm_ref.at[:, q, d], dmk.at[q, :, kept_slot(q, d)], mks.at[q, rel]
+                )
+            )
+            keeps[-1].start()
+
+    item, _ = ranks_at(len_ref, owners[0], tok, (tok, 8), 0)
+    picks = (item == lax.broadcasted_iota(jnp.int32, (tok, 8), 1)).astype(bf16)
+    gamma_one = per_token(picks, table(GAMMA_ONE))
+    resid = x_ref[...].astype(f32) + gamma_one * branch_ref[...]
+    normal, rstd = norm_parts(resid)
+    scale = per_token(picks, table(SCALE_TWO))
+    grad_final = g_ref[...].astype(f32)
+    swaps[0].wait()
+    second = mine_ref[0] + got[0].astype(f32)
+    mid = grad_final + norm_back(normal, rstd, second * (1.0 + scale))
+    tg_ref[...] = mid
+    attn = (gamma_one * mid).astype(bf16)
+    awide[0] = attn
+    swaps[2].start()
+    pay[...] = jnp.zeros_like(pay)
+
+    def put_items(which, values):
+        pay[:, which * D : (which + 1) * D] = per_item(picks, values)
+
+    put_items(SCALE_TWO, second * normal)
+    put_items(SHIFT_TWO, second)
+    put_items(GAMMA_ONE, mid * branch_ref[...])
+    swaps[1].wait()
+    mlp_branch = mine_ref[1] + got[1].astype(f32) + db_ref[...]
+    out_ref[...] = (resid + per_token(picks, table(GAMMA_TWO)) * mlp_branch).astype(bf16)
+    put_items(GAMMA_TWO, grad_final * mlp_branch)
+    row_six = SEGS
+    pay[row_six : row_six + 1, :D] = jnp.sum(attn.astype(f32), axis=0, keepdims=True)
+    pay[row_six : row_six + 1, D : 2 * D] = jnp.sum(
+        gm_ref[...].astype(f32), axis=0, keepdims=True
+    )
+    pay[row_six : row_six + 1, 2 * D :] = hist_ref[...]
+    row = pl.ds(SEGS + 1, 1)
+    for z in range(nz):
+        at = pl.multiple_of((p.core * nz + z) * units, LANES)
+        pay[row, pl.ds(at, units)] = dbias_ref[z : z + 1, :]
+    part[:, :, chunk:] = jnp.zeros((n, 8, LANES), f32)
+
+    lists = seen_lists(steps, tok)
+    for qi in range(CORES):
+        item, rank = ranks_at(len_ref, owners[qi], tok, (8, tok), 1)
+        lo, hi = item[:1] * 16, rank[:1]
+        for j, b in enumerate(lists[qi]):
+            _, e = ranks_at(len_ref, owners[b], tok, (tok, LANES), 0)
+            e = e[:, :1]
+            masks[qi, j] = jnp.where((e >= lo) & (e <= hi), 0.0, -1e30).astype(bf16)
+
+    def proj_rows(s):
+        if merge == 1:
+            return wp[s]
+        return jnp.concatenate([wp[s * merge + i] for i in range(merge)], axis=0)
+
+    def weight(s, k, count=1):
+        at = lambda i, j: normed[((s * merge + i) * 3 + j) * width : ((s * merge + i) * 3 + j + 1) * width, :]
+        if merge == 1:
+            return normed[(s * 3 + k) * width : (s * 3 + k + count) * width, :]
+        rows_of = [at(i, k + j) for j in range(count) for i in range(merge)]
+        return jnp.concatenate(rows_of, axis=0)
+
+    def put_grad(s, k, value):
+        for i in range(merge):
+            da[s * merge + i, k * width : (k + 1) * width, :] = value[
+                i * width : (i + 1) * width
+            ].astype(bf16)
+
+    loads[0].wait()
+    loads[1].wait()
+    swaps[2].wait()
+
+    @pl.loop(0, pairs * CORES)
+    def _(it):
+        s, qi = it // CORES, lax.rem(it, CORES)
+        slot = lax.rem(s, 2)
+
+        @pl.when(qi == 0)
+        def _():
+            for c in fetch(s, slot):
+                c.wait()
+
+            @pl.when(s + 1 < pairs)
+            def _():
+                for c in fetch(s + 1, 1 - slot):
+                    c.start()
+
+            k = ks_[slot]
+            unit = k * lax.rsqrt(half_sums(k * k) + epsilon)
+            ku[...] = unit.astype(bf16)
+            kut[...] = unit.T.astype(bf16)
+            dk[...] = jnp.zeros_like(dk)
+            dv[...] = jnp.zeros_like(dv)
+
+        at = pl.ds(pl.multiple_of(qi * tok, tok), tok)
+        ehs = ehs_ref[s]
+        q = qs_[slot, at, :]
+        rq = lax.rsqrt(half_sums(q * q) + epsilon)
+        qhat = q * rq
+        qu = (qhat * ehs).astype(bf16)
+        qs = [one_half(qu, h) for h in range(2)]
+        g = dot(awide[qi], proj_rows(s), 1, 1).astype(bf16)
+        gs_h = [one_half(g, h) for h in range(2)]
+        turned = (g.astype(f32) * os_[slot, at, :].astype(f32)).T
+        deltas = [
+            jnp.sum(turned[:HEAD], axis=0, keepdims=True),
+            jnp.sum(turned[HEAD:], axis=0, keepdims=True),
+        ]
+        invs = [1.0 / l_ref[s, h : h + 1, at] for h in range(2)]
+        dqt = [None, None]
+        for j in range(len(lists[0])):
+            b = block_at(lists, qi, j)
+            cols = pl.ds(pl.multiple_of(b * tok, tok), tok)
+            mask = masks[qi, j].astype(f32)
+            kb, vb = ku[cols, :], vs_[slot, cols, :]
+            dvs, dks = None, None
+            for h in range(2):
+                w = jnp.exp(dot(kb, qs[h], 1, 1) + mask) * invs[h]
+                dp = dot(vb, gs_h[h], 1, 1)
+                ds = (w * (dp - deltas[h])).astype(bf16)
+                a = dot(w.astype(bf16), gs_h[h])
+                c = dot(ds, qs[h])
+                dvs = a if h == 0 else dvs + a
+                dks = c if h == 0 else dks + c
+                r = dot(kut[h * HEAD : (h + 1) * HEAD, cols], ds)
+                dqt[h] = r if dqt[h] is None else dqt[h] + r
+            dv[cols, :] += dvs
+            dk[cols, :] += dks
+        d = jnp.concatenate(dqt, axis=0).T
+        hsum = jnp.sum(d * qhat * ehs, axis=0, keepdims=True)
+        gq = (ehs * rq * (d - qhat * half_sums(qhat * d))).astype(bf16)
+        gqs[s, at, :] = gq
+        qsum = jnp.sum(gq.astype(f32), axis=0, keepdims=True)
+        qcol = pl.ds(pl.multiple_of(nz * CORES * units + p.core * nz * width + s * LANES, LANES), LANES)
+        vcol = pl.ds(
+            pl.multiple_of(
+                nz * CORES * (units + width) + p.core * nz * width + s * LANES, LANES
+            ),
+            LANES,
+        )
+        pay[row, qcol] += qsum
+        for i in range(merge):
+            chip = (s * merge + i) * CORES + p.core
+            part[chip, SEGS + 1 : SEGS + 2, chunk : chunk + width] += hsum[
+                :, i * width : (i + 1) * width
+            ]
+
+        @pl.when(qi == CORES - 1)
+        def _():
+            k = ks_[slot]
+            rk = lax.rsqrt(half_sums(k * k) + epsilon)
+            khat = k * rk
+            d = dk[...]
+            gkv[s, :, :LANES] = (rk * (d - khat * half_sums(khat * d))).astype(bf16)
+            gv = dv[...].astype(bf16)
+            gkv[s, :, LANES:] = gv
+            pay[row, vcol] = jnp.sum(gv.astype(f32), axis=0, keepdims=True)
+            put_grad(s, 0, dot(gqs[s], normed[:t, :], 0, 0))
+            kvg = dot(gkv[s], normed[: blocks * tok, :], 0, 0)
+            put_grad(s, 1, kvg[:LANES])
+            put_grad(s, 2, kvg[LANES:])
+            both = dot(os_[slot, :tok, :], awide[0], 0, 0)
+            both = both + dot(os_[slot, tok:, :], awide[1], 0, 0)
+            put_grad(s, 3, both)
+
+    def norm_grad(b):
+        at = pl.ds(b * tok, tok)
+        total = None
+        for s in range(pairs):
+            r = dot(gkv[s, at, :], weight(s, 1, 2))
+            if b < CORES:
+                r = r + dot(gqs[s, at, :], weight(s, 0))
+            total = r if total is None else total + r
+        return total
+
+    wloads = [
+        pltpu.make_async_copy(
+            wa_hbm.at[c, pl.ds(0, 3 * width)],
+            normed.at[pl.ds(c * 3 * width, 3 * width)],
+            wl.at[c],
+        )
+        for c in range(nz)
+    ]
+    for c in wloads:
+        c.start()
+    rooms = [awide.at[0], awide.at[1], got.at[0], got.at[1]]
+    rooms += [spare.at[i] for i in range(spare.shape[0])]
+    swap_at = lambda i: rooms[i]
+    for c in wloads:
+        c.wait()
+    gcopies = [
+        remote(swap_at(i), gmine.at[i], gs.at[i], gr.at[i], p.twin()) for i in range(rounds + 1)
+    ]
+    for i in range(rounds, -1, -1):
+        swap_at(i)[...] = norm_grad(2 * i + 1).astype(bf16)
+        gcopies[i].start()
+    for c in keeps:
+        c.wait()
+    rm.advance(0)
+    for chip in range(nz):
+        ra.send_plane(0, chip)
     moves = []
     for i, per_core in enumerate(steps):
+        own = norm_grad(2 * i + 2)
         gcopies[i + 1].wait()
-        gmine[i + 1] = (gn_ref[i + 1, 0] + gmine[i + 1].astype(f32)).astype(bf16)
+        gmine[i + 1] = (own + gmine[i + 1].astype(f32)).astype(bf16)
         for c, step in enumerate(per_core):
             if step is None:
                 continue
             go = (p.core == c) & (p.z - step >= 0) & (p.z - step < nz)
-            got = (p.core == c) & (p.z + step >= 0) & (p.z + step < nz)
-            copy = remote(gmine.at[i + 1], ghalo.at[i], hs.at[i, c], hr.at[i, c], p.on_chip(-step))
+            have = (p.core == c) & (p.z + step >= 0) & (p.z + step < nz)
+            to = (p.dp, jnp.clip(p.z - step, 0, nz - 1) * CORES + p.core)
+            copy = remote(gmine.at[i + 1], ghalo.at[i], hs.at[i, c], hr.at[i, c], to)
             pl.when(go)(copy.start)
-            moves.append((i, go, got, copy))
+            moves.append((i, go, have, copy))
+    own = norm_grad(0)
     gcopies[0].wait()
-    first = gn_ref[0, 0] + gmine[0].astype(f32)
-    tg_ref[...] = first
-    for i, go, got, copy in moves:
-
-        @pl.when(got)
+    own = own + gmine[0].astype(f32)
+    for level in range(1, m):
+        rm.advance(level)
+    for i, go, have, copy in moves:
+        pl.when(have)(copy.wait_recv)
+    for i in range(rounds):
+        any_have = p.core < 0
+        for j, go, have, copy in moves:
+            if j == i:
+                any_have = any_have | have
+
+        @pl.when(jnp.logical_not(any_have))
         def _():
-            copy.wait_recv()
-            tg_ref[...] += ghalo[i].astype(f32)
-
-    first = tg_ref[...]
-    picks = picks_of(seg_ref[...])
+            ghalo[i] = jnp.zeros((tok, D), bf16)
+
+    first = own
+    for i in range(rounds):
+        first = first + ghalo[i].astype(f32)
     normal, rstd = norm_parts(x_ref[...].astype(f32))
-    scale = per_token(picks, mod_ref[SCALE_ONE])
-    tg_ref[...] = mid_ref[...] + norm_back(normal, rstd, first * (1.0 + scale))
-    part[...] = part_ref[...]
-    chunk = 6 * D // n
+    scale = per_token(picks, table(SCALE_ONE))
+    tg_ref[...] += norm_back(normal, rstd, first * (1.0 + scale))
     for which, values in ((SCALE_ONE, first * normal), (SHIFT_ONE, first)):
-        items = per_item(picks, values)
-        begin, end = which * D, (which + 1) * D
-        for j in range(n):
-            a, b = max(begin, j * chunk), min(end, (j + 1) * chunk)
-            if a < b:
-                part[j, :, a - j * chunk : b - j * chunk] += items[:, a - begin : b - begin]
+        pay[:SEGS, which * D : (which + 1) * D] = per_item(picks, values)[:SEGS]
+    for j in range(n):
+        part[j, :, :chunk] = pay[:, j * chunk : (j + 1) * chunk]
     line = p.line()
     sums = [remote(part.at[q[1]], held.at[o], s1.at[o], r1.at[o], q) for o, q in enumerate(line)]
     for c in sums:
         c.start()
-
-    def advance(r, level):
-        for o in far:
-            r.add_plane(level, o)
-            if level + 1 < m:
-                r.send_plane(level + 1, o)
-            elif o:
-                r.send_line(o)
-
-    advance(rm, 0)
-    for o in far:
-        ra.send_plane(0, o)
+    ra.advance(0)
     for c in sums:
         c.wait()
     total = part[p.me] + extra_ref[...]
@@ -1129,17 +1196,14 @@
     for c in sums:
         c.start()
     for level in range(1, m):
-        advance(rm, level)
+        ra.advance(level)
     for c in sums:
         c.wait()
     mine = small_ref.at[p.core, p.z]
     sums = [remote(mine, mine, s3.at[o], r3.at[o], p.on_chip(o)) for o in p.far]
     for c in sums:
         c.start()
-    advance(ra, 0)
     rm.end_line()
-    for level in range(1, m):
-        advance(ra, level)
     for c in sums:
         c.wait()
     mine = small_ref.at[p.core]
@@ -1152,52 +1216,88 @@
     last.wait()
     rm.end()
     ra.end()
-    for i, go, got, copy in moves:
+    for i, go, have, copy in moves:
         pl.when(go)(copy.wait_send)
 
 
-def finish(dm, da, gn, tokens, mid, seg, mod, part, extra, steps, nd):
-    n, rows, cols = part.shape
+def backward(
+    lengths, mine, theirs, tokens, out_grad, gmlp, branch, mod, down_bias, dbias, hist, extra, l,
+    ehs, dm, normed, q, k, v, o, wa, steps, nd, width,
+):
+    n = wa.shape[0] * CORES
     nz = n // CORES
     tok = tokens.shape[0]
     rounds = len(steps)
-    piece, arows = dm.shape[3], da.shape[2]
+    t, w = CORES * tok, k.shape[1]
+    pairs = k.shape[0]
+    piece, arows = dm.shape[3], 4 * width // nd
+    rows, cols = extra.shape
+    seen = len(seen_lists(steps, tok)[0])
     dma = pltpu.SemaphoreType.DMA
     vmem = pl.BlockSpec(memory_space=pltpu.VMEM)
+    anywhere = pl.BlockSpec(memory_space=pl.ANY)
     m = bits_of(nd)
-    levels = max(1, nd // 2)
-    plane = (2, m, nz, levels)
-    wide = lambda: [
+    scr = pltpu.VMEM
+    plane = (2, m, nz, max(1, nd // 2))
+    sems = lambda: [
         dma(plane),
         dma(plane),
         dma((2, nz)),
         dma((2, nz)),
         dma((2, nd)),
         dma((2, nd)),
+        dma((2,)),
     ]
     return pl.pallas_call(
-        functools.partial(finish_body, n, nd, steps),
+        functools.partial(backward_body, n, nd, steps, width),
         out_shape=[
+            jax.ShapeDtypeStruct((tok, D), bf16),
             jax.ShapeDtypeStruct(dm.shape[1:], bf16),
-            jax.ShapeDtypeStruct(da.shape[1:], bf16),
+            jax.ShapeDtypeStruct((4 * width, D), bf16),
             jax.ShapeDtypeStruct((tok, D), f32),
             jax.ShapeDtypeStruct((CORES, nz, nd, rows, cols), f32),
         ],
-        in_specs=[vmem] * 9,
-        out_specs=[vmem] * 4,
+        in_specs=[pl.BlockSpec(memory_space=pltpu.SMEM)] + [vmem] * 13 + [anywhere] * 7,
+        out_specs=[vmem, anywhere, anywhere, vmem, vmem],
         scratch_shapes=[
-            pltpu.VMEM((2, nd - 1, nz, piece, D), bf16),
-            pltpu.VMEM((2, nd - 1, nz, arows, D // 2), bf16),
-            pltpu.VMEM((2, nz, piece, D), bf16),
-            pltpu.VMEM((2, nz, arows, D // 2), bf16),
-            pltpu.VMEM((rounds + 1, tok, D), bf16),
-            pltpu.VMEM((rounds + 1, tok, D), bf16),
-            pltpu.VMEM((rounds, tok, D), bf16),
-            pltpu.VMEM((n, rows, cols), f32),
-            pltpu.VMEM((n - 1, rows, cols), f32),
+            scr((2, tok, D), bf16),
+            scr((CORES, tok, D), bf16),
+            scr((max(1, rounds - 3), tok if rounds > 3 else 16, D), bf16),
+            scr((max(w, pairs * 3 * LANES), D), bf16),
+            scr((nz, width, D), bf16),
+            scr((2, t, LANES), f32),
+            scr((2, w, LANES), f32),
+            scr((2, w, LANES), bf16),
+            scr((2, t, LANES), bf16),
+            scr((w, LANES), bf16),
+            scr((LANES, w), bf16),
+            scr((w, LANES), f32),
+            scr((w, LANES), f32),
+            scr((pairs, t, LANES), bf16),
+            scr((pairs, w, 2 * LANES), bf16),
+            scr((CORES, seen, tok, tok), bf16),
+            scr((2, nz, max(1, nd // 2), piece, D), bf16),
+            scr((2, nd - 1, nz, piece, D), bf16),
+            scr((2, nz - 1, piece, D), bf16),
+            scr((2, piece, D), bf16),
+            scr((nz, 4 * width, D), bf16),
+            scr((2, nd - 1, nz, arows, D // 2), bf16),
+            scr((2, nz - 1, arows, D // 2), bf16),
+            scr((2, arows, D // 2), bf16),
+            scr((rounds + 1, tok, D), bf16),
+            scr((rounds, tok, D), bf16),
+            scr((8, 6 * D), f32),
+            scr((n, rows, cols), f32),
+            scr((n - 1, rows, cols), f32),
+            dma((3,)),
+            dma((3,)),
+            dma((2,)),
+            dma((nz,)),
+            dma((4, 2)),
+            dma((2, nd)),
         ]
-        + wide()
-        + wide()
+        + sems()
+        + sems()
         + [
             dma((rounds + 1,)),
             dma((rounds + 1,)),
@@ -1213,10 +1313,13 @@
             dma,
         ],
         compiler_params=pltpu.CompilerParams(
-            collective_id=3, has_side_effects=True, vmem_limit_bytes=VMEM_LIMIT
+            collective_id=1, has_side_effects=True, vmem_limit_bytes=60 << 20
         ),
-        name="finish",
-    )(dm, da, gn, tokens, mid, seg, mod, part, extra)
+        name="backward",
+    )(
+        lengths, mine, theirs, tokens, out_grad, gmlp, branch, mod, down_bias, dbias, hist, extra,
+        l, ehs, dm, normed, q, k, v, o, wa,
+    )
 
 
 def local(
@@ -1293,55 +1396,12 @@
         item_lengths[0], tokens, out_grad, part, extra, abias, proj_bias[None], apack, mpack,
         steps, nd, width,
     )
-    mod = mod_wide.reshape(8, 6, D).transpose(1, 0, 2)
-
-    segment, scale_ids = item_layout(item_lengths[0])
-    rank = segment * 16 + scale_ids
-    owners = []
-    for s in [(0, 0)] + steps:
-        for flip in range(CORES):
-            c = core ^ flip
-            step = jnp.where(c == 0, nz if s[0] is None else s[0], nz if s[1] is None else s[1])
-            chip = z - step
-            owners.append(jnp.where((chip >= 0) & (chip < nz), chip * CORES + c, -1))
-    blocks = len(owners)
-    seg_blocks, rank_blocks = segment.reshape(nt, tok), rank.reshape(nt, tok)
-    take = lambda a, o: lax.dynamic_index_in_dim(a, jnp.maximum(o, 0), 0, keepdims=False)
-    seg_win = jnp.concatenate([take(seg_blocks, o) for o in owners])
-    e_win = jnp.concatenate([jnp.where(o >= 0, take(rank_blocks, o), -1) for o in owners])
-    lo = seg_win[: CORES * tok] * 16
-    hi = e_win[: CORES * tok]
-    e_blocks = e_win.reshape(blocks, tok)
-    e_max, e_min = jnp.max(e_blocks, axis=1), jnp.min(e_blocks, axis=1)
-    need = (
-        (e_max[None, :] >= jnp.min(lo.reshape(CORES, tok), axis=1)[:, None])
-        & (e_min[None, :] <= jnp.max(hi.reshape(CORES, tok), axis=1)[:, None])
-        & (e_max[None, :] >= 0)
-    ).astype(jnp.int32).reshape(CORES * blocks)
-    seg_own = seg_win[:tok, None]
-
-    merge = nz // pairs
-    weights = (
-        wattn.reshape(pairs, merge, 4, width, D)
-        .transpose(0, 2, 1, 3, 4)
-        .reshape(pairs, 4 * LANES, D)
-    )
-
     up_own = lax.dynamic_index_in_dim(
         up_bias.reshape(nz, CORES, units), core, 1, keepdims=False
     )
-    mlp_part, gx_part, dmlp, dbias = mlp(
+    mine, theirs, dmlp, dbias = mlp(
         nwide.reshape(CORES * tok, D), gwide.reshape(CORES * tok, D), wmlp, up_own
     )
-    mid, awide, heads_grad, layer_out, items, sums = turn(
-        gx_part, mlp_part, resid, branch, out_grad, seg_own, mod, down_bias[None], weights,
-        gwide, nt, nd,
-    )
-    dattn, gn, head_sums = attend_back(
-        need, q_raw, k_raw, v_in, heads_grad, heads_out, weight_sums, ehs, lo[None, :],
-        hi[None, :], e_win[:, None], normed, awide.reshape(CORES * tok, D), weights, tok,
-    )
-
     low_codes = 64
     hot = lambda v, k: (v[:, None] == jnp.arange(k, dtype=jnp.int32)[None, :]).astype(bf16)
     hist = dot(
@@ -1349,46 +1409,12 @@
         hot(token_codes % low_codes, low_codes),
         0,
         0,
-    ).reshape(NBINS)
-    row_six = jnp.concatenate([sums[0], sums[1], hist])
-    to_all = lambda v: jnp.where(
-        (jnp.arange(CORES) == core)[None, :, None], v[:, None, :], 0.0
-    ).reshape(-1)
-    row_seven = jnp.concatenate(
-        [
-            to_all(dbias.reshape(nz, units)),
-            to_all(head_sums[:, 0].reshape(nz, width)),
-            to_all(head_sums[:, 1].reshape(nz, width)),
-        ]
-    )
-    hs_part = to_all(jnp.sum(head_sums[:, 2].reshape(nz, heads, HEAD), axis=2)).reshape(nt, heads)
-    none = jnp.zeros((SEGS, D), f32)
-    mod_part = jnp.concatenate(
-        [items[0, :SEGS], items[1, :SEGS], none, items[2, :SEGS], none, items[3, :SEGS]], axis=1
-    )
-    payload = jnp.concatenate([mod_part, row_six[None], row_seven[None]], axis=0)
-    payload = payload.reshape(8, nt, chunk).transpose(1, 0, 2)
-    tail = jnp.pad(hs_part[:, None, :], ((0, 0), (7, 0), (0, LANES - heads)))
-    own_tail = jnp.pad(
-        cond_act.astype(f32), ((0, 8 - SEGS), (chunk, LANES - feat))
-    )
-    dattn = (
-        dattn.reshape(pairs, 4, merge, width, D)
-        .transpose(0, 2, 1, 3, 4)
-        .reshape(nz, nd, 4 * width // nd, D)
-    )
-    ymlp, yattn, tokens_grad, small = finish(
-        dmlp,
-        dattn,
-        gn.reshape(rounds + 1, CORES, tok, D),
-        tokens,
-        mid,
-        seg_own,
-        mod,
-        jnp.concatenate([payload, tail], axis=2),
-        own_tail,
-        steps,
-        nd,
+    ).reshape(1, NBINS)
+    own_tail = jnp.pad(cond_act.astype(f32), ((0, 8 - SEGS), (chunk, LANES - feat)))
+    layer_out, ymlp, yattn, tokens_grad, small = backward(
+        item_lengths[0], mine, theirs, tokens, out_grad, gwide[0], branch, mod_wide,
+        down_bias[None], dbias.reshape(nz, units), hist, own_tail, weight_sums, ehs, dmlp,
+        normed, q_raw, k_raw, v_in, heads_out, wattn, steps, nd, width,
     )
 
     rows_all = small[..., :chunk].transpose(2, 3, 1, 0, 4).reshape(nd, 8, 6 * D)
@@ -1398,18 +1424,17 @@
     own_small = lax.dynamic_index_in_dim(small, core, 0, keepdims=False)
     own_small = lax.dynamic_index_in_dim(own_small, z, 0, keepdims=False)
     cond_all = own_small[:, :SEGS, chunk : chunk + feat].reshape(nd * SEGS, feat)
-    hscale_grad = jnp.sum(own_small[:, 7, chunk : chunk + heads], axis=0)
+    hscale_grad = jnp.sum(own_small[:, 7, chunk : chunk + width].reshape(nd, heads, HEAD), axis=(0, 2))
     adaw_grad = dot(cond_all, mod_all, 0, 0, highest)
     adab_grad = jnp.sum(mod_all, axis=0)
     cond_grad = dot(mod_own, ada_weight.astype(f32), 1, 1, highest)
     embed_grad = jax.vjp(jax.nn.silu, class_embed)[1](cond_grad[None])[0]
     projb_grad, downb_grad = bias_sums[0, :D], bias_sums[0, D : 2 * D]
     code_hist = bias_sums[0, 2 * D :]
-    at = lambda base, k: lax.dynamic_slice_in_dim(bias_sums[1], base + t * k, k, 0)
+    at = lambda base, k: lax.dynamic_slice_in_dim(bias_sums[1], base + (core * nz + z) * k, k, 0)
     upb_grad = at(0, units)
     qbias_grad = at(nt * units, width)
     vbias_grad = at(nt * (units + width), width)
-    yattn = yattn.reshape(4 * width, D)
     qkvw_grad = yattn[: 3 * width].astype(f32).reshape(3, width, D).transpose(2, 0, 1)
     projw_grad = yattn[3 * width :].astype(f32)
     upw_grad = ymlp[0].reshape(units, D).astype(f32).T

time: 438 us -> 411 us (0.938)
  the two profiles are of different devices: /device:TPU:0 before, /device:TPU:26 now
where the time goes in v1:
time: 411 us; the launch traced here: 406 us
  Pallas kernels  368 us (90%)
  local copies, waits for them, and re-layouts  19.5 us (5%)
  other arithmetic  10.2 us (2%)
  matrix products  6.43 us (2%)
    pallas_call x1, Pallas kernels, backward(): pl.pallas_call(functools.partial(backward_body, n, nd, steps, width), out...  208 us
    pallas_call x1, Pallas kernels, forward(): pl.pallas_call(functools.partial(forward_body, n, nd, steps, width), out_...  138 us
    pallas_call x1, Pallas kernels, mlp(): pl.pallas_call(mlp_body, grid=(steps,), in_specs=[whole(t, D), whole(t, D...  23.2 us

profile of v1, /device:TPU:26, one launch (start us, length us, event | category | flops | bytes accessed | tf_op | source)
XLA Modules:
  0.0 405.8 jit_solution(13088697518406969478)
XLA Ops:
  0.7 0.7 reshape.94
  2.0 1.5 copy.46
  3.5 2.9 pad_maximum_fusion.mpack_ref
  6.4 0.9 copy.52
  7.8 0.7 pad.17.part_ref
  8.8 1.0 pad_maximum_fusion.1.apack_ref
  9.9 0.7 pad.19.abias_ref
  11.4 137.5 %forward.1 = (bf16[1536,1024]{1,0:T(8,128)(2,1)}, f32[4,512,128]{2,1,0:T(8,128)}, f32[4,1536,128]{2,1,0:T(8,128)}, bf16[4,1536,128]{2,1,0:T(8,128)(2,1)}, bf16[4...) custom-call(s32[6]{0:T(128)} %bitcast.90, ...), custom_call_target="tpu_custom_call" | custom-call | tf_op jit(solution)/shard_map/forward/pallas_call | solution.py:627
  149.0 23.2 %mlp.1 = (f32[2,256,1024]{2,1,0:T(8,128)}, bf16[2,256,1024]{2,1,0:T(8,128)(2,1)}, bf16[4,2,4,128,1024]{4,3,2,1,0:T(8,128)(2,1)}, f32[8,1,256]{2,1,0:T(1,128)}) custom-call(bf16[512,1024]{1,0:T(8,128)(2,1)} %bitcast.80, bf16[512,1024]{1,0:T(8,128)(2,1)} %bitcast.77, bf16[4,2,4,128,1024]{4,3,2,1,0:T(8,128)(2,1)} %get-tuple-element.40.w_ref, f32[8,1,256]{2,1,0:T(1,128)} %bitcast.84), custom_call_target="tpu_custom_call" | custom-call | tf_op jit(solution)/shard_map/mlp/pallas_call | solution.py:738
  172.2 0.7 reduce.3
  173.5 0.8 slice_bitcast_fusion.1.gm_ref
  174.6 0.7 reshape.97.hist_ref
  176.0 207.8 %backward.1 = (bf16[256,1024]{1,0:T(8,128)(2,1)}, bf16[2,4,128,1024]{3,2,1,0:T(8,128)(2,1)}, bf16[512,1024]{1,0:T(8,128)(2,1)}, f32[256,1024]{1,0:T(8,128)}, f32[2,4,4,8,896]{4,3,2,1,0:T(8,128)}) custom-call(s32[6]{0:T(128)} %bitcast.91, f32[2,256,1024]{2,1,0:T(8,128)} %get-tuple-element.41.mine_ref, bf16[2,256,1024]{2,1,0:T(8,128)(2,1)} %get-tuple-element.42.theirs_ref, ...), custom_call_target="tpu_custom_call" | custom-call | tf_op jit(solution)/shard_map/backward/pallas_call | solution.py:1251
  383.7 1.7 fusion.23
  385.4 1.9 bitcast_convert_fusion
  387.3 1.8 copy.50
  390.6 4.3 %convolution_bitcast_fusion = f32[128,6144]{1,0:T(8,128)} fusion(f32[4,8,6144]{2,1,0:T(8,128)S(1)} %reshape.98, f32[4,8,896]{2,1,0:T(8,128)S(1)} %dynamic-slice_bitcast_fusion.2), kind=kOutput, calls=%fused_computation | convolution fusion | flops 226492416 | bytes 3948544 | tf_op jit(solution)/shard_map/dot_general | solution.py:31
  397.4 0.7 slice_reduce_fusion
  398.1 1.3 fusion.15
  400.0 1.4 copy.49
  401.5 0.8 slice_convert_fusion
  402.3 0.7 slice_reduce_fusion.2
  403.8 0.8 copy.93
  404.6 1.0 copy.94
  (63 shorter events, 8.9 us)
Async XLA Ops:
  3.5 2.9 copy-start
  6.4 0.9 copy-start.10
  7.3 1.3 copy-start.6
  7.3 1.5 copy-start.8
  7.8 2.1 copy-start.11
  8.5 2.1 copy-start.15
  8.5 2.2 copy-start.13
  8.5 2.2 copy-start.14
  148.9 24.6 %copy-start.2 = (bf16[2,256,1024]{2,1,0:T(8,128)(2,1)S(1)}, bf16[2,256,1024]{2,1,0:T(8,128)(2,1)}, u32[]{:S(2)}) copy-start(bf16[2,256,1024]{2,1,0:T(8,128)(2,1)} %get-tuple-element.39) | copy-start | bytes 3145732
  149.0 25.4 %copy-start.12 = (s32[256]{0:T(256)S(1)}, s32[256]{0:T(256)}, u32[]{:S(2)}) copy-start(s32[256]{0:T(256)} %param.20) | copy-start | bytes 3076
  387.3 1.8 copy-start.5
  390.5 4.4 %copy-start.9 = (f32[4,8,896]{2,1,0:T(8,128)}, f32[4,8,896]{2,1,0:T(8,128)S(1)}, u32[]{:S(2)}) copy-start(f32[4,8,896]{2,1,0:T(8,128)S(1)} %dynamic-slice_bitcast_fusion.2) | copy-start | bytes 344068
  390.5 7.5 %copy-start.1 = (bf16[128,6144]{1,0:T(8,128)(2,1)S(1)}, bf16[128,6144]{1,0:T(8,128)(2,1)}, u32[]{:S(2)}) copy-start(bf16[128,6144]{1,0:T(8,128)(2,1)} %param.21) | copy-start | bytes 4718596
  394.9 5.1 %copy-start.3 = (bf16[512,1024]{1,0:T(8,128)(2,1)S(1)}, bf16[512,1024]{1,0:T(8,128)(2,1)}, u32[]{:S(2)}) copy-start(bf16[512,1024]{1,0:T(8,128)(2,1)} %get-tuple-element.58) | copy-start | bytes 3145732
  400.0 3.8 copy-start.7
  400.0 4.5 %copy-start.4 = (f32[256,1024]{1,0:T(8,128)S(1)}, f32[256,1024]{1,0:T(8,128)}, u32[]{:S(2)}) copy-start(f32[256,1024]{1,0:T(8,128)} %get-tuple-element.119) | copy-start | bytes 3145732

commit v2 on v1

--- a/solution.py
+++ b/solution.py
@@ -512,6 +512,8 @@
     for i in range(rounds):
         twins[i + 1].wait()
 
+    ml.got(1, lambda w, chip: m_spread(w, 1, chip).begin())
+
     @pl.loop(CORES, blocks)
     def _(b):
         norm_block(b)
@@ -522,12 +524,14 @@
         outs.append(pltpu.make_async_copy(src, dst, out_sem.at[i + 1]))
         outs[-1].start()
 
-    ml.got(1, lambda w, chip: m_spread(w, 1, chip).begin())
     trips = pairs * CORES
     agenda = {}
     for step in range(1, nz):
+        if step + 1 < nz:
+            at = min(trips - 1, ((step - 1) * trips) // nz)
+            agenda.setdefault(at, []).append((step + 1, 0))
         at = min(trips - 1, (step * trips) // nz)
-        agenda.setdefault(at, []).append(step)
+        agenda.setdefault(at, []).append((0, step))
 
     @pl.loop(0, trips)
     def _(it):
@@ -567,10 +571,11 @@
 
             @pl.when(it == when)
             def _():
-                for step in todo:
-                    if step + 1 < nz:
-                        ml.got(step + 1, lambda w, chip: m_spread(w, step + 1, chip).begin())
-                    ml.each(step, lambda w, chip: m_spread(w, step, chip).step(0))
+                for get, step in todo:
+                    if get:
+                        ml.got(get, lambda w, chip: m_spread(w, get, chip).begin())
+                    else:
+                        ml.each(step, lambda w, chip: m_spread(w, step, chip).step(0))
 
     def project(at):
         total = dot(o_ref[0, at, :], weight(0, 3))
@@ -729,7 +734,7 @@
     t = x.shape[0]
     tok = t // CORES
     nz, _, nd, piece, _ = weights.shape
-    count = min(nd, max(1, 256 // piece))
+    count = min(nd, max(1, 512 // piece))
     per = nd // count
     steps, units = nz * per, count * piece
     whole = lambda *shape: pl.BlockSpec(shape, lambda i: (0,) * len(shape))
@@ -816,8 +821,11 @@
             if level + 1 < self.m:
                 self.send_plane(level + 1, self.p.chip(o))
             elif o:
-                for _, c in self.line(o):
-                    c.start()
+                self.send_line(o)
+
+    def send_line(self, o):
+        for _, c in self.line(o):
+            c.start()
 
     def end_line(self):
         p = self.p
@@ -910,7 +918,8 @@
     swaps.append(remote(awide.at[0], awide.at[1], xs.at[2], xr.at[2], p.twin()))
     swaps[0].start()
     swaps[1].start()
-    for o in far:
+    early = far[: nz // 2]
+    for o in early:
         rm.send_plane(0, p.chip(o))
     loads = [
         pltpu.make_async_copy(wa_hbm.at[:, pl.ds(3 * width, width)], wp, load.at[0]),
@@ -1005,9 +1014,36 @@
                 i * width : (i + 1) * width
             ].astype(bf16)
 
-    loads[0].wait()
-    loads[1].wait()
+    for c in loads + keeps:
+        c.wait()
     swaps[2].wait()
+
+    trips = pairs * CORES
+    agenda = {}
+
+    def at_trip(it, do):
+        agenda.setdefault(min(it, trips - 1), []).append(do)
+
+    def pass_on(level, o):
+        rm.add_plane(level, p.chip(o))
+        if level + 1 < m:
+            rm.send_plane(level + 1, p.chip(o))
+        elif o:
+            rm.send_line(o)
+
+    per_trip = max(1, nz // 4)
+    for k, o in enumerate(early):
+        at_trip(1 + k // per_trip, functools.partial(pass_on, 0, o))
+        if k + len(early) < nz:
+            at_trip(
+                1 + k // per_trip,
+                functools.partial(rm.send_plane, 0, p.chip(far[k + len(early)])),
+            )
+    if m > 1:
+        for k, o in enumerate(early):
+            at_trip(5 + k // per_trip, functools.partial(pass_on, 1, o))
+    late = far[len(early) :]
+    at_trip(6, functools.partial(pass_on, 0, late[0]))
 
     @pl.loop(0, pairs * CORES)
     def _(it):
@@ -1102,6 +1138,13 @@
             both = both + dot(os_[slot, tok:, :], awide[1], 0, 0)
             put_grad(s, 3, both)
 
+        for when, todo in agenda.items():
+
+            @pl.when(it == when)
+            def _():
+                for do in todo:
+                    do()
+
     def norm_grad(b):
         at = pl.ds(b * tok, tok)
         total = None
@@ -1133,11 +1176,10 @@
     for i in range(rounds, -1, -1):
         swap_at(i)[...] = norm_grad(2 * i + 1).astype(bf16)
         gcopies[i].start()
-    for c in keeps:
-        c.wait()
-    rm.advance(0)
-    for chip in range(nz):
-        ra.send_plane(0, chip)
+    for o in late[1:]:
+        pass_on(0, o)
+    for o in far[: nz // 2]:
+        ra.send_plane(0, p.chip(o))
     moves = []
     for i, per_core in enumerate(steps):
         own = norm_grad(2 * i + 2)
@@ -1155,8 +1197,21 @@
     own = norm_grad(0)
     gcopies[0].wait()
     own = own + gmine[0].astype(f32)
-    for level in range(1, m):
-        rm.advance(level)
+    if m > 1:
+        for o in late:
+            pass_on(1, o)
+    for level in range(2, m):
+        for o in far:
+            pass_on(level, o)
+    for o in far[nz // 2 :]:
+        ra.send_plane(0, p.chip(o))
+    rm.end_line()
+    for o in far[: nz // 2]:
+        ra.add_plane(0, p.chip(o))
+        if m > 1:
+            ra.send_plane(1, p.chip(o))
+        elif o:
+            ra.send_line(o)
     for i, go, have, copy in moves:
         pl.when(have)(copy.wait_recv)
     for i in range(rounds):
@@ -1183,7 +1238,12 @@
     sums = [remote(part.at[q[1]], held.at[o], s1.at[o], r1.at[o], q) for o, q in enumerate(line)]
     for c in sums:
         c.start()
-    ra.advance(0)
+    for o in far[nz // 2 :]:
+        ra.add_plane(0, p.chip(o))
+        if m > 1:
+            ra.send_plane(1, p.chip(o))
+        elif o:
+            ra.send_line(o)
     for c in sums:
         c.wait()
     total = part[p.me] + extra_ref[...]
@@ -1203,15 +1263,16 @@
     sums = [remote(mine, mine, s3.at[o], r3.at[o], p.on_chip(o)) for o in p.far]
     for c in sums:
         c.start()
-    rm.end_line()
+    rm.back.step(0)
+    ra.end_line()
     for c in sums:
         c.wait()
     mine = small_ref.at[p.core]
     last = remote(mine, mine, s4, r4, p.twin())
     last.start()
-    ra.end_line()
     for level in range(m):
-        rm.back.step(level)
+        if level:
+            rm.back.step(level)
         ra.back.step(level)
     last.wait()
     rm.end()

time: 411 us -> 366 us (0.89)
  the two profiles are of different devices: /device:TPU:26 before, /device:TPU:0 now
where the time goes in v2:
time: 366 us; the launch traced here: 361 us
  Pallas kernels  324 us (89%)
  local copies, waits for them, and re-layouts  20.3 us (6%)
  other arithmetic  9.46 us (3%)
  matrix products  6.43 us (2%)
    pallas_call x1, Pallas kernels, backward(): pl.pallas_call(functools.partial(backward_body, n, nd, steps, width), out...  183 us
    pallas_call x1, Pallas kernels, forward(): pl.pallas_call(functools.partial(forward_body, n, nd, steps, width), out_...  120 us
    pallas_call x1, Pallas kernels, mlp(): pl.pallas_call(mlp_body, grid=(steps,), in_specs=[whole(t, D), whole(t, D...  20.7 us

profile of v2, /device:TPU:0, one launch (start us, length us, event | category | flops | bytes accessed | tf_op | source)
XLA Modules:
  0.0 361.1 jit_solution(16349574981499037544)
XLA Ops:
  0.7 0.7 reshape.91
  2.0 1.5 copy.46
  3.5 2.9 pad_maximum_fusion.mpack_ref
  6.4 0.9 copy.52
  7.8 0.7 pad.17.part_ref
  8.8 1.0 pad_maximum_fusion.1.apack_ref
  9.9 0.7 pad.19.abias_ref
  11.4 119.5 %forward.1 = (bf16[1536,1024]{1,0:T(8,128)(2,1)}, f32[4,512,128]{2,1,0:T(8,128)}, f32[4,1536,128]{2,1,0:T(8,128)}, bf16[4,1536,128]{2,1,0:T(8,128)(2,1)}, bf16[4...) custom-call(s32[6]{0:T(128)} %bitcast.92, ...), custom_call_target="tpu_custom_call" | custom-call | tf_op jit(solution)/shard_map/forward/pallas_call | solution.py:632
  131.0 20.7 %mlp.1 = (f32[2,256,1024]{2,1,0:T(8,128)}, bf16[2,256,1024]{2,1,0:T(8,128)(2,1)}, bf16[4,2,4,128,1024]{4,3,2,1,0:T(8,128)(2,1)}, f32[4,1,512]{2,1,0:T(1,128)}) custom-call(bf16[512,1024]{1,0:T(8,128)(2,1)} %bitcast.82, bf16[512,1024]{1,0:T(8,128)(2,1)} %bitcast.79, bf16[4,2,4,128,1024]{4,3,2,1,0:T(8,128)(2,1)} %get-tuple-element.40.w_ref, ...), custom_call_target="tpu_custom_call" | custom-call | tf_op jit(solution)/shard_map/mlp/pallas_call | solution.py:743
  151.7 1.3 copy.93
  153.0 0.8 slice_bitcast_fusion.1.gm_ref
  154.2 0.7 reshape.93.hist_ref
  155.5 183.5 %backward.1 = (bf16[256,1024]{1,0:T(8,128)(2,1)}, bf16[2,4,128,1024]{3,2,1,0:T(8,128)(2,1)}, bf16[512,1024]{1,0:T(8,128)(2,1)}, f32[256,1024]{1,0:T(8,128)}, f32[2,4,4,8,896]{4,3,2,1,0:T(8,128)}) custom-call(s32[6]{0:T(128)} %bitcast.93, f32[2,256,1024]{2,1,0:T(8,128)} %get-tuple-element.41.mine_ref, bf16[2,256,1024]{2,1,0:T(8,128)(2,1)} %get-tuple-element.42.theirs_ref, ...), custom_call_target="tpu_custom_call" | custom-call | tf_op jit(solution)/shard_map/backward/pallas_call | solution.py:1312
  339.0 1.7 fusion.23
  340.7 1.9 bitcast_convert_fusion
  342.6 2.0 copy.50
  345.9 4.3 %convolution_bitcast_fusion = f32[128,6144]{1,0:T(8,128)} fusion(f32[4,8,6144]{2,1,0:T(8,128)S(1)} %reshape.94, f32[4,8,896]{2,1,0:T(8,128)S(1)} %dynamic-slice_bitcast_fusion.2), kind=kOutput, calls=%fused_computation | convolution fusion | flops 226492416 | bytes 3948544 | tf_op jit(solution)/shard_map/dot_general | solution.py:31
  352.8 0.7 slice_reduce_fusion
  353.4 1.3 fusion.15
  355.4 1.4 copy.49
  356.8 0.8 slice_convert_fusion
  357.7 0.7 slice_reduce_fusion.2
  359.2 0.8 copy.96
  359.9 1.0 copy.97
  (62 shorter events, 8.3 us)
Async XLA Ops:
  3.5 2.9 copy-start
  6.4 0.9 copy-start.10
  7.3 1.3 copy-start.6
  7.3 1.5 copy-start.8
  7.8 2.1 copy-start.11
  8.5 2.1 copy-start.15
  8.5 2.2 copy-start.13
  8.5 2.2 copy-start.14
  131.0 22.1 %copy-start.2 = (bf16[2,256,1024]{2,1,0:T(8,128)(2,1)S(1)}, bf16[2,256,1024]{2,1,0:T(8,128)(2,1)}, u32[]{:S(2)}) copy-start(bf16[2,256,1024]{2,1,0:T(8,128)(2,1)} %get-tuple-element.39) | copy-start | bytes 3145732
  131.0 22.9 %copy-start.12 = (s32[256]{0:T(256)S(1)}, s32[256]{0:T(256)}, u32[]{:S(2)}) copy-start(s32[256]{0:T(256)} %param.20) | copy-start | bytes 3076
  342.6 2.0 copy-start.5
  345.9 4.3 %copy-start.9 = (f32[4,8,896]{2,1,0:T(8,128)}, f32[4,8,896]{2,1,0:T(8,128)S(1)}, u32[]{:S(2)}) copy-start(f32[4,8,896]{2,1,0:T(8,128)S(1)} %dynamic-slice_bitcast_fusion.2) | copy-start | bytes 344068
  345.9 7.5 %copy-start.1 = (bf16[128,6144]{1,0:T(8,128)(2,1)S(1)}, bf16[128,6144]{1,0:T(8,128)(2,1)}, u32[]{:S(2)}) copy-start(bf16[128,6144]{1,0:T(8,128)(2,1)} %param.21) | copy-start | bytes 4718596
  350.3 5.1 %copy-start.3 = (bf16[512,1024]{1,0:T(8,128)(2,1)S(1)}, bf16[512,1024]{1,0:T(8,128)(2,1)}, u32[]{:S(2)}) copy-start(bf16[512,1024]{1,0:T(8,128)(2,1)} %get-tuple-element.58) | copy-start | bytes 3145732
  355.4 3.8 %copy-start.7 = (bf16[256,1024]{1,0:T(8,128)(2,1)S(1)}, bf16[256,1024]{1,0:T(8,128)(2,1)}, u32[]{:S(2)}) copy-start(bf16[256,1024]{1,0:T(8,128)(2,1)} %get-tuple-element.118) | copy-start | bytes 1572868
  355.4 4.5 %copy-start.4 = (f32[256,1024]{1,0:T(8,128)S(1)}, f32[256,1024]{1,0:T(8,128)}, u32[]{:S(2)}) copy-start(f32[256,1024]{1,0:T(8,128)} %get-tuple-element.119) | copy-start | bytes 3145732

commit v3 on v2

--- a/solution.py
+++ b/solution.py
@@ -77,6 +77,9 @@
 
     def on_chip(self, step):
         return (self.dp, self.chip(step) * CORES + self.core)
+
+    def turn(self, k):
+        return jnp.where(self.z < self.nz // 2, self.nz - 1 - k, k)
 
     def twin(self):
         return (self.dp, self.z * CORES + 1 - self.core)
@@ -758,9 +761,9 @@
 
 
 class Reduce:
-    def __init__(self, place, sent, kept, stage, zstage, final, out, sems):
+    def __init__(self, place, sent, kept, stage, zstage, out, sems):
         self.p, self.sent, self.kept = place, sent, kept
-        self.stage, self.zstage, self.final = stage, zstage, final
+        self.stage, self.zstage = stage, zstage
         self.ps, self.pr, self.zs, self.zr, self.os, self.or_, self.fs = sems
         self.m = bits_of(place.nd)
         self.back = Spread(place, out, self.os, self.or_)
@@ -805,41 +808,75 @@
                 mine = self.current(part, level, chip, rel)
                 room[...] = (room[...].astype(f32) + mine[...].astype(f32)).astype(bf16)
 
-    def line(self, o):
-        for part in range(2):
-            yield part, remote(
-                self.stage(part, self.m - 1, self.p.chip(o), 0),
-                self.zstage(part, o),
-                self.zs.at[part, o],
-                self.zr.at[part, o],
-                self.p.on_chip(o),
+    def hop(self, chip):
+        p = self.p
+        right = chip > p.z
+        way, room = jnp.where(right, 0, 1), jnp.abs(chip - p.z)
+        to = (p.dp, jnp.clip(jnp.where(right, p.z + 1, p.z - 1), 0, p.nz - 1) * CORES + p.core)
+        behind = (chip != p.z) & jnp.where(right, p.z > 0, p.z < p.nz - 1)
+        before = jnp.maximum(room - 1, 0)
+        copies = [
+            remote(
+                self.stage(part, self.m - 1, chip, 0),
+                self.zstage(part, way, before),
+                self.zs.at[part, way, before],
+                self.zr.at[part, way, before],
+                to,
             )
-
-    def advance(self, level, then=None):
-        for o in self.p.far + [0]:
-            self.add_plane(level, self.p.chip(o))
-            if level + 1 < self.m:
-                self.send_plane(level + 1, self.p.chip(o))
-            elif o:
-                self.send_line(o)
-
-    def send_line(self, o):
-        for _, c in self.line(o):
-            c.start()
+            for part in range(2)
+        ]
+        return copies, behind, way, jnp.minimum(room, p.nz - 2)
+
+    def arrive(self, part, way, room):
+        p = self.p
+        ref = self.zstage(part, way, room)
+        remote(ref, ref, self.zs.at[part, way, room], self.zr.at[part, way, room], p.twin()).wait_recv()
+
+    def send_line(self, chip):
+        copies, behind, _, _ = self.hop(chip)
+
+        @pl.when((chip != self.p.z) & jnp.logical_not(behind))
+        def _():
+            for c in copies:
+                c.start()
+
+    def forward_line(self, chip):
+        copies, behind, way, room = self.hop(chip)
+
+        @pl.when(behind)
+        def _():
+            for part, c in enumerate(copies):
+                self.arrive(part, way, room)
+                mine = self.stage(part, self.m - 1, chip, 0)
+                got = self.zstage(part, way, room)
+                mine[...] = (mine[...].astype(f32) + got[...].astype(f32)).astype(bf16)
+                c.start()
+
+    def pass_on(self, level, chip):
+        self.add_plane(level, chip)
+        if level + 1 < self.m:
+            self.send_plane(level + 1, chip)
+        else:
+            self.send_line(chip)
 
     def end_line(self):
         p = self.p
-        for o in p.far:
-            for _, c in self.line(o):
-                c.wait_recv()
         puts = []
+        for way, there in ((0, p.z > 0), (1, p.z < p.nz - 1)):
+
+            @pl.when(there)
+            def _():
+                for part in range(2):
+                    self.arrive(part, way, 0)
+                    mine = self.stage(part, self.m - 1, p.z, 0)
+                    got = self.zstage(part, way, 0)
+                    mine[...] = (mine[...].astype(f32) + got[...].astype(f32)).astype(bf16)
+
         for part in range(2):
-            total = self.stage(part, self.m - 1, p.z, 0)[...].astype(f32)
-            for o in p.far:
-                total = total + self.zstage(part, o)[...].astype(f32)
-            self.final(part)[...] = total.astype(bf16)
             puts.append(
-                pltpu.make_async_copy(self.final(part), self.out(part, p.dp), self.fs.at[part])
+                pltpu.make_async_copy(
+                    self.stage(part, self.m - 1, p.z, 0), self.out(part, p.dp), self.fs.at[part]
+                )
             )
             puts[-1].start()
         for c in puts:
@@ -851,9 +888,14 @@
             for chip in range(self.p.nz):
                 for c in self.plane(level, chip):
                     c.wait_send()
-        for o in self.p.far:
-            for _, c in self.line(o):
-                c.wait_send()
+        for chip in range(self.p.nz):
+            copies, _, _, _ = self.hop(chip)
+
+            @pl.when(chip != self.p.z)
+            def _():
+                for c in copies:
+                    c.wait_send()
+
         self.back.end()
 
 
@@ -863,7 +905,7 @@
     o_hbm, wa_hbm,
     out_ref, ym_ref, ya_ref, tg_ref, small_ref,
     got, awide, spare, normed, wp, qs_, ks_, vs_, os_, ku, kut, dk, dv, gqs, gkv, masks,
-    dmk, mstage, mz, mfinal, da, astage, az, afinal, gmine, ghalo, pay, part, held,
+    dmk, mstage, mz, da, astage, az, gmine, ghalo, pay, part, held,
     xs, xr, load, wl, ld, mks,
     mps, mpr, mzs, mzr, mos, mor, mfs, aps, apr, azs, azr, aos, aor, afs,
     gs, gr, hs, hr, s1, r1, s2, r2, s3, r3, s4, r4,
@@ -896,8 +938,7 @@
         lambda q, chip, d: dm_ref.at[chip, q, d],
         lambda q, chip, d: dmk.at[q, chip, kept_slot(q, d)],
         lambda q, level, chip, slot: mstage.at[q, base(level) + slot, chip],
-        lambda q, o: mz.at[q, o - 1],
-        lambda q: mfinal.at[q],
+        lambda q, way, room: mz.at[q, way, room],
         lambda q, d: ym_ref.at[q, d],
         (mps, mpr, mzs, mzr, mos, mor, mfs),
     )
@@ -907,20 +948,19 @@
         a_own,
         a_own,
         lambda q, level, chip, slot: astage.at[q, base(level) + slot, chip],
-        lambda q, o: az.at[q, o - 1],
-        lambda q: afinal.at[q],
+        lambda q, way, room: az.at[q, way, room],
         lambda q, d: ya_ref.at[pl.ds(d * arows, arows), cut(q)],
         (aps, apr, azs, azr, aos, aor, afs),
     )
     p.greet_all()
-    far = p.far + [0]
+    far = [p.turn(k) for k in range(nz)]
     swaps = [remote(theirs_ref.at[i], got.at[i], xs.at[i], xr.at[i], p.twin()) for i in range(2)]
     swaps.append(remote(awide.at[0], awide.at[1], xs.at[2], xr.at[2], p.twin()))
     swaps[0].start()
     swaps[1].start()
     early = far[: nz // 2]
     for o in early:
-        rm.send_plane(0, p.chip(o))
+        rm.send_plane(0, o)
     loads = [
         pltpu.make_async_copy(wa_hbm.at[:, pl.ds(3 * width, width)], wp, load.at[0]),
         pltpu.make_async_copy(n_hbm, normed.at[pl.ds(0, blocks * tok)], load.at[1]),
@@ -1024,26 +1064,22 @@
     def at_trip(it, do):
         agenda.setdefault(min(it, trips - 1), []).append(do)
 
-    def pass_on(level, o):
-        rm.add_plane(level, p.chip(o))
-        if level + 1 < m:
-            rm.send_plane(level + 1, p.chip(o))
-        elif o:
-            rm.send_line(o)
-
     per_trip = max(1, nz // 4)
     for k, o in enumerate(early):
-        at_trip(1 + k // per_trip, functools.partial(pass_on, 0, o))
+        at_trip(1 + k // per_trip, functools.partial(rm.pass_on, 0, o))
         if k + len(early) < nz:
             at_trip(
                 1 + k // per_trip,
-                functools.partial(rm.send_plane, 0, p.chip(far[k + len(early)])),
+                functools.partial(rm.send_plane, 0, far[k + len(early)]),
             )
     if m > 1:
         for k, o in enumerate(early):
-            at_trip(5 + k // per_trip, functools.partial(pass_on, 1, o))
+            at_trip(4 + k // per_trip, functools.partial(rm.pass_on, 1, o))
     late = far[len(early) :]
-    at_trip(6, functools.partial(pass_on, 0, late[0]))
+    at_trip(5, functools.partial(rm.pass_on, 0, late[0]))
+    if nz == 4 and m == 2:
+        at_trip(7, functools.partial(rm.pass_on, 0, late[1]))
+        at_trip(6, functools.partial(rm.forward_line, early[0]))
 
     @pl.loop(0, pairs * CORES)
     def _(it):
@@ -1177,9 +1213,12 @@
         swap_at(i)[...] = norm_grad(2 * i + 1).astype(bf16)
         gcopies[i].start()
     for o in late[1:]:
-        pass_on(0, o)
+        if not (nz == 4 and m == 2):
+            rm.pass_on(0, o)
     for o in far[: nz // 2]:
-        ra.send_plane(0, p.chip(o))
+        ra.send_plane(0, o)
+    if m == 2 and nz != 4:
+        rm.forward_line(early[0])
     moves = []
     for i, per_core in enumerate(steps):
         own = norm_grad(2 * i + 2)
@@ -1199,19 +1238,17 @@
     own = own + gmine[0].astype(f32)
     if m > 1:
         for o in late:
-            pass_on(1, o)
+            rm.pass_on(1, o)
     for level in range(2, m):
         for o in far:
-            pass_on(level, o)
+            rm.pass_on(level, o)
     for o in far[nz // 2 :]:
-        ra.send_plane(0, p.chip(o))
-    rm.end_line()
+        ra.send_plane(0, o)
+    for k, o in enumerate(far):
+        if k or m != 2:
+            rm.forward_line(o)
     for o in far[: nz // 2]:
-        ra.add_plane(0, p.chip(o))
-        if m > 1:
-            ra.send_plane(1, p.chip(o))
-        elif o:
-            ra.send_line(o)
+        ra.pass_on(0, o)
     for i, go, have, copy in moves:
         pl.when(have)(copy.wait_recv)
     for i in range(rounds):
@@ -1239,30 +1276,30 @@
     for c in sums:
         c.start()
     for o in far[nz // 2 :]:
-        ra.add_plane(0, p.chip(o))
-        if m > 1:
-            ra.send_plane(1, p.chip(o))
-        elif o:
-            ra.send_line(o)
+        ra.pass_on(0, o)
     for c in sums:
         c.wait()
     total = part[p.me] + extra_ref[...]
     for o in range(n - 1):
         total = total + held[o]
-    small_ref[p.core, p.z, p.dp] = total
-    mine = small_ref.at[p.core, p.z, p.dp]
+    small_ref[p.core, p.dp, p.z] = total
+    mine = small_ref.at[p.core, p.dp, p.z]
+    sums = [remote(mine, mine, s3.at[o], r3.at[o], p.on_chip(o)) for o in p.far]
+    for c in sums:
+        c.start()
+    for level in range(1, m):
+        for o in far:
+            ra.pass_on(level, o)
+    for c in sums:
+        c.wait()
+    mine = small_ref.at[p.core, p.dp]
     plane = [(lax.rem(p.dp + o, nd), p.me) for o in range(1, nd)]
     sums = [remote(mine, mine, s2.at[o], r2.at[o], q) for o, q in enumerate(plane)]
     for c in sums:
         c.start()
-    for level in range(1, m):
-        ra.advance(level)
-    for c in sums:
-        c.wait()
-    mine = small_ref.at[p.core, p.z]
-    sums = [remote(mine, mine, s3.at[o], r3.at[o], p.on_chip(o)) for o in p.far]
-    for c in sums:
-        c.start()
+    rm.end_line()
+    for o in far:
+        ra.forward_line(o)
     rm.back.step(0)
     ra.end_line()
     for c in sums:
@@ -1303,8 +1340,8 @@
     sems = lambda: [
         dma(plane),
         dma(plane),
-        dma((2, nz)),
-        dma((2, nz)),
+        dma((2, 2, nz)),
+        dma((2, 2, nz)),
         dma((2, nd)),
         dma((2, nd)),
         dma((2,)),
@@ -1316,7 +1353,7 @@
             jax.ShapeDtypeStruct(dm.shape[1:], bf16),
             jax.ShapeDtypeStruct((4 * width, D), bf16),
             jax.ShapeDtypeStruct((tok, D), f32),
-            jax.ShapeDtypeStruct((CORES, nz, nd, rows, cols), f32),
+            jax.ShapeDtypeStruct((CORES, nd, nz, rows, cols), f32),
         ],
         in_specs=[pl.BlockSpec(memory_space=pltpu.SMEM)] + [vmem] * 13 + [anywhere] * 7,
         out_specs=[vmem, anywhere, anywhere, vmem, vmem],
@@ -1339,12 +1376,10 @@
             scr((CORES, seen, tok, tok), bf16),
             scr((2, nz, max(1, nd // 2), piece, D), bf16),
             scr((2, nd - 1, nz, piece, D), bf16),
-            scr((2, nz - 1, piece, D), bf16),
-            scr((2, piece, D), bf16),
+            scr((2, 2, nz - 1, piece, D), bf16),
             scr((nz, 4 * width, D), bf16),
             scr((2, nd - 1, nz, arows, D // 2), bf16),
-            scr((2, nz - 1, arows, D // 2), bf16),
-            scr((2, arows, D // 2), bf16),
+            scr((2, 2, nz - 1, arows, D // 2), bf16),
             scr((rounds + 1, tok, D), bf16),
             scr((rounds, tok, D), bf16),
             scr((8, 6 * D), f32),
@@ -1478,12 +1513,12 @@
         normed, q_raw, k_raw, v_in, heads_out, wattn, steps, nd, width,
     )
 
-    rows_all = small[..., :chunk].transpose(2, 3, 1, 0, 4).reshape(nd, 8, 6 * D)
+    rows_all = small[..., :chunk].transpose(1, 3, 2, 0, 4).reshape(nd, 8, 6 * D)
     mod_all = rows_all[:, :SEGS].reshape(nd * SEGS, 6 * D)
     mod_own = lax.dynamic_index_in_dim(rows_all, d, 0, keepdims=False)[:SEGS]
     bias_sums = jnp.sum(rows_all[:, SEGS:], axis=0)
     own_small = lax.dynamic_index_in_dim(small, core, 0, keepdims=False)
-    own_small = lax.dynamic_index_in_dim(own_small, z, 0, keepdims=False)
+    own_small = lax.dynamic_index_in_dim(own_small, z, 1, keepdims=False)
     cond_all = own_small[:, :SEGS, chunk : chunk + feat].reshape(nd * SEGS, feat)
     hscale_grad = jnp.sum(own_small[:, 7, chunk : chunk + width].reshape(nd, heads, HEAD), axis=(0, 2))
     adaw_grad = dot(cond_all, mod_all, 0, 0, highest)

time: 366 us -> 347 us (0.948)
  Pallas kernels: 324 us -> 305 us
    pallas_call x1, Pallas kernels: 183 us -> 165 us  [backward(): pl.pallas_call(functools.partial(backward_body, n, nd, steps, width), out...]
where the time goes in v3:
time: 347 us; the launch traced here: 342 us
  Pallas kernels  305 us (88%)
  local copies, waits for them, and re-layouts  20.2 us (6%)
  other arithmetic  9.46 us (3%)
  matrix products  6.43 us (2%)
    pallas_call x1, Pallas kernels, backward(): pl.pallas_call(functools.partial(backward_body, n, nd, steps, width), out...  165 us
    pallas_call x1, Pallas kernels, forward(): pl.pallas_call(functools.partial(forward_body, n, nd, steps, width), out_...  120 us
    pallas_call x1, Pallas kernels, mlp(): pl.pallas_call(mlp_body, grid=(steps,), in_specs=[whole(t, D), whole(t, D...  20.7 us

profile of v3, /device:TPU:0, one launch (start us, length us, event | category | flops | bytes accessed | tf_op | source)
XLA Modules:
  0.0 342.4 jit_solution(5712357402242189138)
XLA Ops:
  0.7 0.7 reshape.91
  2.0 1.5 copy.46
  3.5 2.9 pad_maximum_fusion.mpack_ref
  6.4 0.9 copy.52
  7.8 0.7 pad.17.part_ref
  8.8 1.0 pad_maximum_fusion.1.apack_ref
  9.9 0.7 pad.19.abias_ref
  11.4 119.6 %forward.1 = (bf16[1536,1024]{1,0:T(8,128)(2,1)}, f32[4,512,128]{2,1,0:T(8,128)}, f32[4,1536,128]{2,1,0:T(8,128)}, bf16[4,1536,128]{2,1,0:T(8,128)(2,1)}, bf16[4...) custom-call(s32[6]{0:T(128)} %bitcast.92, ...), custom_call_target="tpu_custom_call" | custom-call | tf_op jit(solution)/shard_map/forward/pallas_call | solution.py:635
  131.0 20.7 %mlp.1 = (f32[2,256,1024]{2,1,0:T(8,128)}, bf16[2,256,1024]{2,1,0:T(8,128)(2,1)}, bf16[4,2,4,128,1024]{4,3,2,1,0:T(8,128)(2,1)}, f32[4,1,512]{2,1,0:T(1,128)}) custom-call(bf16[512,1024]{1,0:T(8,128)(2,1)} %bitcast.82, bf16[512,1024]{1,0:T(8,128)(2,1)} %bitcast.79, bf16[4,2,4,128,1024]{4,3,2,1,0:T(8,128)(2,1)} %get-tuple-element.40.w_ref, ...), custom_call_target="tpu_custom_call" | custom-call | tf_op jit(solution)/shard_map/mlp/pallas_call | solution.py:746
  151.8 1.3 copy.93
  153.1 0.8 slice_bitcast_fusion.1.gm_ref
  154.2 0.7 reshape.93.hist_ref
  155.5 164.9 %backward.1 = (bf16[256,1024]{1,0:T(8,128)(2,1)}, bf16[2,4,128,1024]{3,2,1,0:T(8,128)(2,1)}, bf16[512,1024]{1,0:T(8,128)(2,1)}, f32[256,1024]{1,0:T(8,128)}, f32[2,4,4,8,896]{4,3,2,1,0:T(8,128)}) custom-call(s32[6]{0:T(128)} %bitcast.93, f32[2,256,1024]{2,1,0:T(8,128)} %get-tuple-element.41.mine_ref, bf16[2,256,1024]{2,1,0:T(8,128)(2,1)} %get-tuple-element.42.theirs_ref, ...), custom_call_target="tpu_custom_call" | custom-call | tf_op jit(solution)/shard_map/backward/pallas_call | solution.py:1349
  320.4 1.7 fusion.23
  322.1 1.9 bitcast_convert_fusion
  324.0 1.8 copy.50
  327.2 4.3 %convolution_bitcast_fusion = f32[128,6144]{1,0:T(8,128)} fusion(f32[4,8,6144]{2,1,0:T(8,128)S(1)} %reshape.94, f32[4,8,896]{2,1,0:T(8,128)S(1)} %dynamic-slice_bitcast_fusion.2), kind=kOutput, calls=%fused_computation | convolution fusion | flops 226492416 | bytes 3948544 | tf_op jit(solution)/shard_map/dot_general | solution.py:31
  334.1 0.7 slice_reduce_fusion
  334.8 1.3 fusion.15
  336.7 1.4 copy.49
  338.2 0.8 slice_convert_fusion
  339.0 0.7 slice_reduce_fusion.2
  340.5 0.8 copy.96
  341.3 1.0 copy.97
  (62 shorter events, 8.3 us)
Async XLA Ops:
  3.5 2.9 copy-start
  6.4 0.9 copy-start.10
  7.3 1.3 copy-start.6
  7.3 1.5 copy-start.8
  7.8 2.1 copy-start.11
  8.5 2.1 copy-start.15
  8.5 2.2 copy-start.13
  8.5 2.2 copy-start.14
  131.0 22.1 %copy-start.2 = (bf16[2,256,1024]{2,1,0:T(8,128)(2,1)S(1)}, bf16[2,256,1024]{2,1,0:T(8,128)(2,1)}, u32[]{:S(2)}) copy-start(bf16[2,256,1024]{2,1,0:T(8,128)(2,1)} %get-tuple-element.39) | copy-start | bytes 3145732
  131.0 22.9 %copy-start.12 = (s32[256]{0:T(256)S(1)}, s32[256]{0:T(256)}, u32[]{:S(2)}) copy-start(s32[256]{0:T(256)} %param.20) | copy-start | bytes 3076
  324.0 1.8 copy-start.5
  327.2 4.4 %copy-start.9 = (f32[4,8,896]{2,1,0:T(8,128)}, f32[4,8,896]{2,1,0:T(8,128)S(1)}, u32[]{:S(2)}) copy-start(f32[4,8,896]{2,1,0:T(8,128)S(1)} %dynamic-slice_bitcast_fusion.2) | copy-start | bytes 344068
  327.2 7.5 %copy-start.1 = (bf16[128,6144]{1,0:T(8,128)(2,1)S(1)}, bf16[128,6144]{1,0:T(8,128)(2,1)}, u32[]{:S(2)}) copy-start(bf16[128,6144]{1,0:T(8,128)(2,1)} %param.21) | copy-start | bytes 4718596
  331.6 5.1 %copy-start.3 = (bf16[512,1024]{1,0:T(8,128)(2,1)S(1)}, bf16[512,1024]{1,0:T(8,128)(2,1)}, u32[]{:S(2)}) copy-start(bf16[512,1024]{1,0:T(8,128)(2,1)} %get-tuple-element.58) | copy-start | bytes 3145732
  336.7 3.8 %copy-start.7 = (bf16[256,1024]{1,0:T(8,128)(2,1)S(1)}, bf16[256,1024]{1,0:T(8,128)(2,1)}, u32[]{:S(2)}) copy-start(bf16[256,1024]{1,0:T(8,128)(2,1)} %get-tuple-element.118) | copy-start | bytes 1572868
  336.7 4.5 %copy-start.4 = (f32[256,1024]{1,0:T(8,128)S(1)}, f32[256,1024]{1,0:T(8,128)}, u32[]{:S(2)}) copy-start(f32[256,1024]{1,0:T(8,128)} %get-tuple-element.119) | copy-start | bytes 3145732

commit v4 on v3

--- a/solution.py
+++ b/solution.py
@@ -162,42 +162,54 @@
         z = self.p.z - self.ways[w] * step
         return jnp.clip(z, 0, self.p.nz - 1), self.inside(z)
 
-    def copy(self, w, step):
+    def copies(self, w, step):
         p = self.p
         to = p.z + self.ways[w]
         chip, have = self.source(w, step - 1)
-        src = self.own if step == 1 else self.ref_of(chip)
-        c = remote(
-            src,
-            self.ref_of(chip),
-            self.send.at[w, step],
-            self.recv.at[w, step],
-            (p.dp, jnp.clip(to, 0, p.nz - 1) * CORES + p.core),
-        )
-        return c, have & self.inside(to)
+        there = self.ref_of(chip)
+        cs = [
+            remote(
+                src,
+                dst,
+                self.send.at[w, step, i],
+                self.recv.at[w, step, i],
+                (p.dp, jnp.clip(to, 0, p.nz - 1) * CORES + p.core),
+            )
+            for i, (src, dst) in enumerate(zip(self.own if step == 1 else there, there))
+        ]
+        return cs, have & self.inside(to)
 
     def start(self, step=1):
         for w in range(2):
-            c, do = self.copy(w, step)
-            pl.when(do)(c.start)
+            cs, do = self.copies(w, step)
+
+            @pl.when(do)
+            def _():
+                for c in cs:
+                    c.start()
 
     def got(self, step, then):
         for w in range(2):
             chip, have = self.source(w, step)
-            to = self.p.z + self.ways[w]
-            ref = self.ref_of(chip)
-            wait = remote(
-                ref, ref, self.send.at[w, step], self.recv.at[w, step], self.p.twin()
-            )
-            on, more = None, None
+            waits = [
+                remote(ref, ref, self.send.at[w, step, i], self.recv.at[w, step, i], self.p.twin())
+                for i, ref in enumerate(self.ref_of(chip))
+            ]
+            on, more = [], None
             if step + 1 < self.p.nz:
-                on, more = self.copy(w, step + 1)
+                on, more = self.copies(w, step + 1)
 
             @pl.when(have)
             def _():
-                wait.wait_recv()
-                if on is not None:
-                    pl.when(more)(on.start)
+                for c in waits:
+                    c.wait_recv()
+                if on:
+
+                    @pl.when(more)
+                    def _():
+                        for c in on:
+                            c.start()
+
                 then(w, chip)
 
     def each(self, step, do):
@@ -208,8 +220,12 @@
     def end(self):
         for step in range(1, self.p.nz):
             for w in range(2):
-                c, do = self.copy(w, step)
-                pl.when(do)(c.wait_send)
+                cs, do = self.copies(w, step)
+
+                @pl.when(do)
+                def _():
+                    for c in cs:
+                        c.wait_send()
 
 
 def picks_of(seg):
@@ -325,8 +341,9 @@
 
 
 def forward_body(
-    n, nd, steps, width, len_ref, tok_ref, grad_ref, part_ref, extra_ref, abias_ref, pb_ref,
-    apack_ref, mpack_ref,
+    n, nd, steps, width, len_ref, hs_ref, tok_ref, grad_ref, part_ref, abias_ref, qbias_ref,
+    vbias_ref, pb_ref,
+    apack_ref, up_ref, down_ref,
     n_out, q_out, k_out, v_out, o_ref, l_ref, wa_out, wm_ref, branch_ref, resid_ref, nwide_ref,
     gwide_ref, mod_ref, ehs_ref,
     win, wa, modc, held, normed, qv, kv, vv, qb, vb, masks, ku, v0, v1, theirs, got,
@@ -348,8 +365,14 @@
 
     a_at = lambda chip, d: wa.at[chip, pl.ds(d * rows, rows)]
     mine = pl.ds(p.dp * rows, rows)
-    al = Line(p, apack_ref.at[mine], lambda chip: wa.at[chip, mine], azs, azr)
-    ml = Line(p, mpack_ref.at[:, p.dp], lambda chip: wm_ref.at[chip, :, p.dp], mzs, mzr)
+    al = Line(p, [apack_ref.at[mine]], lambda chip: [wa.at[chip, mine]], azs, azr)
+    ml = Line(
+        p,
+        [up_ref.at[p.dp], down_ref.at[p.dp]],
+        lambda chip: [wm_ref.at[chip, i, p.dp] for i in range(2)],
+        mzs,
+        mzr,
+    )
 
     def a_spread(w, step, chip):
         return Spread(
@@ -368,7 +391,8 @@
     owns = [
         pltpu.make_async_copy(tok_ref, win.at[0], local_sem.at[0]),
         pltpu.make_async_copy(apack_ref, wa.at[p.z], local_sem.at[1]),
-        pltpu.make_async_copy(mpack_ref, wm_ref.at[p.z], local_sem.at[2]),
+        pltpu.make_async_copy(up_ref, wm_ref.at[p.z, 0], local_sem.at[2]),
+        pltpu.make_async_copy(down_ref, wm_ref.at[p.z, 1], local_sem.at[3]),
     ]
     for c in owns:
         c.start()
@@ -384,10 +408,16 @@
     twins[0].start()
     for c in sums:
         c.wait()
-    total = part_ref[p.me] + extra_ref[...] + abias_ref[p.me]
+    own = pl.ds(pl.multiple_of(p.me * chunk, LANES), chunk)
+    total = part_ref[p.me] + abias_ref[:, own]
     for o in range(n - 1):
         total = total + held[o]
     modc[p.me] = total
+    modc[p.me, SEGS : SEGS + 1, :width] = qbias_ref[...]
+    modc[p.me, SEGS : SEGS + 1, width : 2 * width] = vbias_ref[...]
+    for h in range(width // HEAD):
+        at = 2 * width + h * HEAD
+        modc[p.me, SEGS : SEGS + 1, at : at + HEAD] = jnp.exp(jnp.full((1, HEAD), hs_ref[h], f32))
     sums = [
         remote(modc.at[p.me], modc.at[p.me], s2.at[o], r2.at[o], q) for o, q in enumerate(line)
     ]
@@ -613,11 +643,15 @@
     for i, go, have, copy in moves:
         pl.when(go)(copy.wait_send)
     owns[2].wait()
+    owns[3].wait()
     for c in outs:
         c.wait()
 
 
-def forward(lengths, tokens, out_grad, part, extra, abias, proj_bias, apack, mpack, steps, nd, width):
+def forward(
+    lengths, scales, tokens, out_grad, part, abias, qbias, vbias, proj_bias, apack, up, down,
+    steps, nd, width,
+):
     n, _, cols = part.shape
     nz = n // CORES
     tok = tokens.shape[0]
@@ -642,7 +676,7 @@
             low(pairs, t, LANES),
             out(pairs, 8, t),
             low(nz, 4 * width, D),
-            low(nz, *mpack.shape),
+            low(nz, 2, *up.shape),
             out(tok, D),
             out(tok, D),
             low(CORES, tok, D),
@@ -650,9 +684,10 @@
             out(8, 6 * D),
             out(pairs, 1, LANES),
         ],
-        in_specs=[pl.BlockSpec(memory_space=pltpu.SMEM), anywhere]
-        + [vmem] * 5
-        + [anywhere] * 2,
+        in_specs=[pl.BlockSpec(memory_space=pltpu.SMEM)] * 2
+        + [anywhere]
+        + [vmem] * 6
+        + [anywhere] * 3,
         out_specs=[anywhere] * 4 + [vmem] * 2 + [anywhere] * 2 + [vmem] * 6,
         scratch_shapes=[
             v((blocks, tok, D), bf16),
@@ -679,11 +714,11 @@
             dma((rounds, CORES)),
             dma((rounds + 1,)),
             dma((rounds + 1,)),
-            dma((2, nz)),
-            dma((2, nz)),
-            dma((2, nz)),
-            dma((2, nz)),
-            dma((3,)),
+            dma((2, nz, 1)),
+            dma((2, nz, 1)),
+            dma((2, nz, 2)),
+            dma((2, nz, 2)),
+            dma((4,)),
             dma((5,)),
             dma((2, nz, 2, nd)),
             dma((2, nz, 2, nd)),
@@ -696,10 +731,12 @@
             collective_id=0, has_side_effects=True, vmem_limit_bytes=VMEM_LIMIT
         ),
         name="forward",
-    )(lengths, tokens, out_grad, part, extra, abias, proj_bias, apack, mpack)
-
-
-def mlp_body(x_ref, g_ref, w_ref, bias_ref, mine_ref, theirs_ref, dw_ref, dbias_ref, mlp, gx):
+    )(
+        lengths, scales, tokens, out_grad, part, abias, qbias, vbias, proj_bias, apack, up, down
+    )
+
+
+def mlp_body(x_ref, g_ref, w_ref, bias_ref, mine_ref, theirs_ref, dw_ref, dbias_ref, gsum_ref, mlp, gx):
     x, g = x_ref[...], g_ref[...]
     tok = mine_ref.shape[1]
     units = w_ref.shape[2] * w_ref.shape[3]
@@ -717,6 +754,7 @@
 
     @pl.when(pl.program_id(0) == 0)
     def _():
+        gsum_ref[...] = jnp.sum(g[:tok].astype(f32), axis=0, keepdims=True)
         mlp[...] = jnp.zeros_like(mlp)
         gx[...] = jnp.zeros_like(gx)
 
@@ -747,12 +785,13 @@
         mlp_body,
         grid=(steps,),
         in_specs=[whole(t, D), whole(t, D), block, row],
-        out_specs=[whole(2, tok, D), whole(2, tok, D), block, row],
+        out_specs=[whole(2, tok, D), whole(2, tok, D), block, row, whole(1, D)],
         out_shape=[
             jax.ShapeDtypeStruct((2, tok, D), f32),
             jax.ShapeDtypeStruct((2, tok, D), bf16),
             jax.ShapeDtypeStruct(weights.shape, bf16),
             jax.ShapeDtypeStruct((steps, 1, units), f32),
+            jax.ShapeDtypeStruct((1, D), f32),
         ],
         scratch_shapes=[pltpu.VMEM((t, D), f32), pltpu.VMEM((t, D), f32)],
         compiler_params=pltpu.CompilerParams(vmem_limit_bytes=VMEM_LIMIT),
@@ -901,7 +940,7 @@
 
 def backward_body(
     n, nd, steps, width, len_ref, mine_ref, theirs_ref, x_ref, g_ref, gm_ref, branch_ref, mod_ref,
-    db_ref, dbias_ref, hist_ref, extra_ref, l_ref, ehs_ref, dm_ref, n_hbm, q_hbm, k_hbm, v_hbm,
+    db_ref, dbias_ref, code_ref, extra_ref, l_ref, ehs_ref, dm_ref, n_hbm, q_hbm, k_hbm, v_hbm,
     o_hbm, wa_hbm,
     out_ref, ym_ref, ya_ref, tg_ref, small_ref,
     got, awide, spare, normed, wp, qs_, ks_, vs_, os_, ku, kut, dk, dv, gqs, gkv, masks,
@@ -1017,10 +1056,15 @@
     put_items(GAMMA_TWO, grad_final * mlp_branch)
     row_six = SEGS
     pay[row_six : row_six + 1, :D] = jnp.sum(attn.astype(f32), axis=0, keepdims=True)
-    pay[row_six : row_six + 1, D : 2 * D] = jnp.sum(
-        gm_ref[...].astype(f32), axis=0, keepdims=True
-    )
-    pay[row_six : row_six + 1, 2 * D :] = hist_ref[...]
+    pay[row_six : row_six + 1, D : 2 * D] = gm_ref[...]
+    codes = code_ref[...]
+    bins = NBINS // LANES
+    high = lax.broadcasted_iota(jnp.int32, (bins, tok), 0) == codes // LANES
+    low = lax.broadcasted_iota(jnp.int32, (LANES, tok), 0) == lax.rem(codes, LANES)
+    counts = dot(high.astype(f32).astype(bf16), low.astype(f32).astype(bf16), 1, 1)
+    for i in range(bins):
+        at = 2 * D + i * LANES
+        pay[row_six : row_six + 1, at : at + LANES] = counts[i : i + 1, :]
     row = pl.ds(SEGS + 1, 1)
     for z in range(nz):
         at = pl.multiple_of((p.core * nz + z) * units, LANES)
@@ -1319,7 +1363,7 @@
 
 
 def backward(
-    lengths, mine, theirs, tokens, out_grad, gmlp, branch, mod, down_bias, dbias, hist, extra, l,
+    lengths, mine, theirs, tokens, out_grad, gmlp, branch, mod, down_bias, dbias, codes, extra, l,
     ehs, dm, normed, q, k, v, o, wa, steps, nd, width,
 ):
     n = wa.shape[0] * CORES
@@ -1355,7 +1399,9 @@
             jax.ShapeDtypeStruct((tok, D), f32),
             jax.ShapeDtypeStruct((CORES, nd, nz, rows, cols), f32),
         ],
-        in_specs=[pl.BlockSpec(memory_space=pltpu.SMEM)] + [vmem] * 13 + [anywhere] * 7,
+        in_specs=[pl.BlockSpec(memory_space=pltpu.SMEM)]
+        + [vmem] * 13
+        + [anywhere] * 7,
         out_specs=[vmem, anywhere, anywhere, vmem, vmem],
         scratch_shapes=[
             scr((2, tok, D), bf16),
@@ -1413,7 +1459,7 @@
         ),
         name="backward",
     )(
-        lengths, mine, theirs, tokens, out_grad, gmlp, branch, mod, down_bias, dbias, hist, extra,
+        lengths, mine, theirs, tokens, out_grad, gmlp, branch, mod, down_bias, dbias, codes, extra,
         l, ehs, dm, normed, q, k, v, o, wa,
     )
 
@@ -1468,48 +1514,28 @@
     cond_act = jax.nn.silu(class_embed[0]).astype(bf16)
     ada_part = jnp.dot(cond_act, ada_weight, preferred_element_type=f32)
     part = jnp.pad(ada_part.reshape(SEGS, nt, chunk).transpose(1, 0, 2), ((0, 0), (0, 2), (0, 0)))
-    bias_row = jnp.concatenate(
-        [
-            query_bias,
-            value_bias,
-            jnp.broadcast_to(jnp.exp(head_scale)[:, None], (heads, HEAD)).reshape(width),
-            jnp.zeros((chunk - 3 * width,), f32),
-        ]
-    )
-    extra = jnp.pad(bias_row[None], ((SEGS, 7 - SEGS), (0, 0)))
-    abias = jnp.pad(
-        jnp.broadcast_to(ada_bias.reshape(nt, 1, chunk), (nt, SEGS, chunk)),
-        ((0, 0), (0, 8 - SEGS), (0, 0)),
-    )
     apack = jnp.concatenate(
         [qkv_weight.transpose(1, 2, 0).reshape(3 * width, D), proj_weight], axis=0
     )
-    mpack = jnp.stack([up_weight.T, down_weight]).reshape(2, nd, units // nd, D)
+    up_pack = up_weight.T.reshape(nd, units // nd, D)
+    down_pack = down_weight.reshape(nd, units // nd, D)
     (
         normed, q_raw, k_raw, v_in, heads_out, weight_sums, wattn, wmlp, branch, resid, nwide,
         gwide, mod_wide, ehs,
     ) = forward(
-        item_lengths[0], tokens, out_grad, part, extra, abias, proj_bias[None], apack, mpack,
-        steps, nd, width,
+        item_lengths[0], head_scale, tokens, out_grad, part, ada_bias[None], query_bias[None],
+        value_bias[None], proj_bias[None], apack, up_pack, down_pack, steps, nd, width,
     )
     up_own = lax.dynamic_index_in_dim(
         up_bias.reshape(nz, CORES, units), core, 1, keepdims=False
     )
-    mine, theirs, dmlp, dbias = mlp(
+    mine, theirs, dmlp, dbias, gsum = mlp(
         nwide.reshape(CORES * tok, D), gwide.reshape(CORES * tok, D), wmlp, up_own
     )
-    low_codes = 64
-    hot = lambda v, k: (v[:, None] == jnp.arange(k, dtype=jnp.int32)[None, :]).astype(bf16)
-    hist = dot(
-        hot(token_codes // low_codes, NBINS // low_codes),
-        hot(token_codes % low_codes, low_codes),
-        0,
-        0,
-    ).reshape(1, NBINS)
     own_tail = jnp.pad(cond_act.astype(f32), ((0, 8 - SEGS), (chunk, LANES - feat)))
     layer_out, ymlp, yattn, tokens_grad, small = backward(
-        item_lengths[0], mine, theirs, tokens, out_grad, gwide[0], branch, mod_wide,
-        down_bias[None], dbias.reshape(nz, units), hist, own_tail, weight_sums, ehs, dmlp,
+        item_lengths[0], mine, theirs, tokens, out_grad, gsum, branch, mod_wide,
+        down_bias[None], dbias.reshape(nz, units), token_codes.reshape(1, tok), own_tail, weight_sums, ehs, dmlp,
         normed, q_raw, k_raw, v_in, heads_out, wattn, steps, nd, width,
     )
 
@@ -1521,9 +1547,9 @@
     own_small = lax.dynamic_index_in_dim(own_small, z, 1, keepdims=False)
     cond_all = own_small[:, :SEGS, chunk : chunk + feat].reshape(nd * SEGS, feat)
     hscale_grad = jnp.sum(own_small[:, 7, chunk : chunk + width].reshape(nd, heads, HEAD), axis=(0, 2))
-    adaw_grad = dot(cond_all, mod_all, 0, 0, highest)
+    adaw_grad = dot(cond_all, mod_all, 0, 0, lax.Precision.HIGH)
     adab_grad = jnp.sum(mod_all, axis=0)
-    cond_grad = dot(mod_own, ada_weight.astype(f32), 1, 1, highest)
+    cond_grad = dot(mod_own, ada_weight.astype(f32), 1, 1, lax.Precision.HIGH)
     embed_grad = jax.vjp(jax.nn.silu, class_embed)[1](cond_grad[None])[0]
     projb_grad, downb_grad = bias_sums[0, :D], bias_sums[0, D : 2 * D]
     code_hist = bias_sums[0, 2 * D :]

time: 347 us -> 340 us (0.980)
  no operation moved by 1% of the time
where the time goes in v4:
time: 340 us; the launch traced here: 335 us
  Pallas kernels  305 us (90%)
  local copies, waits for them, and re-layouts  18.1 us (5%)
  other arithmetic  6.58 us (2%)
  matrix products  4.51 us (1%)
    pallas_call x1, Pallas kernels, backward(): pl.pallas_call(functools.partial(backward_body, n, nd, steps, width), out...  165 us
    pallas_call x1, Pallas kernels, forward(): pl.pallas_call(functools.partial(forward_body, n, nd, steps, width), out_...  120 us
    pallas_call x1, Pallas kernels, mlp(): pl.pallas_call(mlp_body, grid=(steps,), in_specs=[whole(t, D), whole(t, D...  20.8 us

profile of v4, /device:TPU:0, one launch (start us, length us, event | category | flops | bytes accessed | tf_op | source)
XLA Modules:
  0.0 335.5 jit_solution(1955290405670438100)
XLA Ops:
  0.7 0.7 reshape.85
  2.0 2.0 copy.52
  4.5 0.7 pad.10.part_ref
  5.5 1.0 pad_maximum_fusion.apack_ref
  6.6 1.3 copy.46
  7.9 119.7 %forward.1 = (bf16[1536,1024]{1,0:T(8,128)(2,1)}, f32[4,512,128]{2,1,0:T(8,128)}, f32[4,1536,128]{2,1,0:T(8,128)}, bf16[4,1536,128]{2,1,0:T(8,128)(2,1)}, bf16[4...) custom-call(s32[6]{0:T(128)} %bitcast.95, ...), custom_call_target="tpu_custom_call" | custom-call | tf_op jit(solution)/shard_map/forward/pallas_call | solution.py:669
  127.6 20.8 %mlp.1 = (f32[2,256,1024]{2,1,0:T(8,128)}, bf16[2,256,1024]{2,1,0:T(8,128)(2,1)}, bf16[4,2,4,128,1024]{4,3,2,1,0:T(8,128)(2,1)}, f32[4,1,512]{2,1,0:T(1,128)}, f32[1,1024]{1,0:T(1,128)}) custom-call(bf16[512,1024]{1,0:T(8,128)(2,1)} %bitcast.84, bf16[512,1024]{1,0:T(8,128)(2,1)} %bitcast.85, bf16[4,2,4,128,1024]{4,3,2,1,0:T(8,128)(2,1)} %get-tuple-element.41.w_ref, ...), custom_call_target="tpu_custom_call" | custom-call | tf_op jit(solution)/shard_map/mlp/pallas_call | solution.py:784
  148.4 1.3 copy.93
  149.7 0.6 pad_convert_fusion.extra_ref
  150.4 164.7 %backward.1 = (bf16[256,1024]{1,0:T(8,128)(2,1)}, bf16[2,4,128,1024]{3,2,1,0:T(8,128)(2,1)}, bf16[512,1024]{1,0:T(8,128)(2,1)}, f32[256,1024]{1,0:T(8,128)}, f32[2,4,4,8,896]{4,3,2,1,0:T(8,128)}) custom-call(s32[6]{0:T(128)} %bitcast.96, f32[2,256,1024]{2,1,0:T(8,128)} %get-tuple-element.42.mine_ref, bf16[2,256,1024]{2,1,0:T(8,128)(2,1)} %get-tuple-element.43.theirs_ref, ...), custom_call_target="tpu_custom_call" | custom-call | tf_op jit(solution)/shard_map/backward/pallas_call | solution.py:1393
  315.1 1.7 fusion.20
  316.8 1.9 bitcast_convert_fusion
  318.7 1.8 copy.50
  321.2 0.6 reshape.88
  321.9 3.1 convolution_bitcast_fusion
  326.2 0.6 slice.69
  327.5 0.7 slice_reduce_fusion
  328.2 0.9 fusion.12
  329.7 1.4 copy.49
  331.2 0.8 slice_convert_fusion
  332.0 0.7 slice_reduce_fusion.2
  332.8 0.6 reduce_sum.38
  333.5 0.8 copy.96
  334.3 1.0 copy.97
  (35 shorter events, 4.7 us)
Async XLA Ops:
  0.6 3.4 %copy-start.9 = (f32[1,6,128]{2,0,1:T(1,128)S(1)}, f32[1,6,128]{2,0,1:T(1,128)}, u32[]{:S(2)}) copy-start(f32[1,6,128]{2,0,1:T(1,128)} %param.18) | copy-start | bytes 9220
  2.0 3.2 copy-start.5
  4.0 1.5 copy-start.7
  4.5 2.1 copy-start.2
  318.7 1.8 copy-start.4
  321.9 3.1 copy-start.8
  321.9 6.3 %copy-start = (bf16[128,6144]{1,0:T(8,128)(2,1)S(1)}, bf16[128,6144]{1,0:T(8,128)(2,1)}, u32[]{:S(2)}) copy-start(bf16[128,6144]{1,0:T(8,128)(2,1)} %param.21) | copy-start | bytes 4718596
  325.0 4.7 %copy-start.1 = (bf16[512,1024]{1,0:T(8,128)(2,1)S(1)}, bf16[512,1024]{1,0:T(8,128)(2,1)}, u32[]{:S(2)}) copy-start(bf16[512,1024]{1,0:T(8,128)(2,1)} %get-tuple-element.60) | copy-start | bytes 3145732
  329.7 3.8 %copy-start.6 = (bf16[256,1024]{1,0:T(8,128)(2,1)S(1)}, bf16[256,1024]{1,0:T(8,128)(2,1)}, u32[]{:S(2)}) copy-start(bf16[256,1024]{1,0:T(8,128)(2,1)} %get-tuple-element.118) | copy-start | bytes 1572868
  329.7 4.5 %copy-start.3 = (f32[256,1024]{1,0:T(8,128)S(1)}, f32[256,1024]{1,0:T(8,128)}, u32[]{:S(2)}) copy-start(f32[256,1024]{1,0:T(8,128)} %get-tuple-element.119) | copy-start | bytes 3145732

commit v5 on v4

--- a/solution.py
+++ b/solution.py
@@ -341,12 +341,12 @@
 
 
 def forward_body(
-    n, nd, steps, width, len_ref, hs_ref, tok_ref, grad_ref, part_ref, abias_ref, qbias_ref,
+    n, nd, steps, width, len_ref, hs_ref, tok_ref, grad_ref, emb_ref, ada_ref, abias_ref, qbias_ref,
     vbias_ref, pb_ref,
     apack_ref, up_ref, down_ref,
     n_out, q_out, k_out, v_out, o_ref, l_ref, wa_out, wm_ref, branch_ref, resid_ref, nwide_ref,
     gwide_ref, mod_ref, ehs_ref,
-    win, wa, modc, held, normed, qv, kv, vv, qb, vb, masks, ku, v0, v1, theirs, got,
+    win, wa, modc, held, part_ref, normed, qv, kv, vv, qb, vb, masks, ku, v0, v1, theirs, got,
     s1, r1, s2, r2, ts, tr, cs, cr, azs, azr, mzs, mzr, local_sem, out_sem, das, dar, dms, dmr,
     ms, mr,
 ):
@@ -396,6 +396,11 @@
     ]
     for c in owns:
         c.start()
+    x = emb_ref[...]
+    cond = (x / (1.0 + jnp.exp(-x))).astype(bf16)
+    part_ref[...] = jnp.zeros_like(part_ref)
+    for j in range(n):
+        part_ref[j, :SEGS, :] = dot(cond, ada_ref[:, j * chunk : (j + 1) * chunk])
     sums = [
         remote(part_ref.at[q[1]], held.at[o], s1.at[o], r1.at[o], q) for o, q in enumerate(line)
     ]
@@ -649,10 +654,10 @@
 
 
 def forward(
-    lengths, scales, tokens, out_grad, part, abias, qbias, vbias, proj_bias, apack, up, down,
-    steps, nd, width,
+    lengths, scales, tokens, out_grad, embed, ada, abias, qbias, vbias, proj_bias, apack, up, down,
+    steps, n, nd, width,
 ):
-    n, _, cols = part.shape
+    part_shape = (n, 8, ada.shape[1] // n)
     nz = n // CORES
     tok = tokens.shape[0]
     rounds = len(steps)
@@ -686,14 +691,15 @@
         ],
         in_specs=[pl.BlockSpec(memory_space=pltpu.SMEM)] * 2
         + [anywhere]
-        + [vmem] * 6
+        + [vmem] * 7
         + [anywhere] * 3,
         out_specs=[anywhere] * 4 + [vmem] * 2 + [anywhere] * 2 + [vmem] * 6,
         scratch_shapes=[
             v((blocks, tok, D), bf16),
             v((nz, 4 * width, D), bf16),
-            v(part.shape, f32),
-            v((n - 1,) + part.shape[1:], f32),
+            v(part_shape, f32),
+            v((n - 1,) + part_shape[1:], f32),
+            v(part_shape, f32),
             v((w, D), bf16),
             v((pairs, t, LANES), f32),
             v((pairs, w, LANES), f32),
@@ -732,7 +738,8 @@
         ),
         name="forward",
     )(
-        lengths, scales, tokens, out_grad, part, abias, qbias, vbias, proj_bias, apack, up, down
+        lengths, scales, tokens, out_grad, embed, ada, abias, qbias, vbias, proj_bias, apack, up,
+        down,
     )
 
 
@@ -956,7 +963,7 @@
     pairs = l_ref.shape[0]
     merge = LANES // width
     arows = 4 * width // nd
-    units = dbias_ref.shape[1]
+    units = dbias_ref.shape[0] * dbias_ref.shape[2] // nz
     t = CORES * tok
     half = D // 2
     m = bits_of(nd)
@@ -1067,8 +1074,10 @@
         pay[row_six : row_six + 1, at : at + LANES] = counts[i : i + 1, :]
     row = pl.ds(SEGS + 1, 1)
     for z in range(nz):
-        at = pl.multiple_of((p.core * nz + z) * units, LANES)
-        pay[row, pl.ds(at, units)] = dbias_ref[z : z + 1, :]
+        per = dbias_ref.shape[0] // nz
+        for i in range(per):
+            at = pl.multiple_of((p.core * nz + z) * units + i * (units // per), LANES)
+            pay[row, pl.ds(at, units // per)] = dbias_ref[z * per + i]
     part[:, :, chunk:] = jnp.zeros((n, 8, LANES), f32)
 
     lists = seen_lists(steps, tok)
@@ -1512,8 +1521,6 @@
 
     chunk = ada_weight.shape[1] // nt
     cond_act = jax.nn.silu(class_embed[0]).astype(bf16)
-    ada_part = jnp.dot(cond_act, ada_weight, preferred_element_type=f32)
-    part = jnp.pad(ada_part.reshape(SEGS, nt, chunk).transpose(1, 0, 2), ((0, 0), (0, 2), (0, 0)))
     apack = jnp.concatenate(
         [qkv_weight.transpose(1, 2, 0).reshape(3 * width, D), proj_weight], axis=0
     )
@@ -1523,8 +1530,9 @@
         normed, q_raw, k_raw, v_in, heads_out, weight_sums, wattn, wmlp, branch, resid, nwide,
         gwide, mod_wide, ehs,
     ) = forward(
-        item_lengths[0], head_scale, tokens, out_grad, part, ada_bias[None], query_bias[None],
-        value_bias[None], proj_bias[None], apack, up_pack, down_pack, steps, nd, width,
+        item_lengths[0], head_scale, tokens, out_grad, class_embed[0], ada_weight, ada_bias[None],
+        query_bias[None], value_bias[None], proj_bias[None], apack, up_pack, down_pack, steps,
+        nt, nd, width,
     )
     up_own = lax.dynamic_index_in_dim(
         up_bias.reshape(nz, CORES, units), core, 1, keepdims=False
@@ -1535,7 +1543,7 @@
     own_tail = jnp.pad(cond_act.astype(f32), ((0, 8 - SEGS), (chunk, LANES - feat)))
     layer_out, ymlp, yattn, tokens_grad, small = backward(
         item_lengths[0], mine, theirs, tokens, out_grad, gsum, branch, mod_wide,
-        down_bias[None], dbias.reshape(nz, units), token_codes.reshape(1, tok), own_tail, weight_sums, ehs, dmlp,
+        down_bias[None], dbias, token_codes.reshape(1, tok), own_tail, weight_sums, ehs, dmlp,
         normed, q_raw, k_raw, v_in, heads_out, wattn, steps, nd, width,
     )
 

time: 340 us -> 338 us (level)
  no operation moved by 1% of the time
where the time goes in v5:
time: 338 us; the launch traced here: 334 us
  Pallas kernels  306 us (91%)
  local copies, waits for them, and re-layouts  15.9 us (5%)
  other arithmetic  7.53 us (2%)
  matrix products  4.01 us (1%)
    pallas_call x1, Pallas kernels, backward(): pl.pallas_call(functools.partial(backward_body, n, nd, steps, width), out...  165 us
    pallas_call x1, Pallas kernels, forward(): pl.pallas_call(functools.partial(forward_body, n, nd, steps, width), out_...  120 us
    pallas_call x1, Pallas kernels, mlp(): pl.pallas_call(mlp_body, grid=(steps,), in_specs=[whole(t, D), whole(t, D...  20.8 us

profile of v5, /device:TPU:0, one launch (start us, length us, event | category | flops | bytes accessed | tf_op | source)
XLA Modules:
  0.0 334.1 jit_solution(7632600637346725346)
XLA Ops:
  0.7 0.8 reshape.79
  1.5 0.6 constant_dynamic-slice_fusion.3.bias_ref
  2.1 1.4 copy.40
  3.5 2.0 pad_maximum_fusion.apack_ref
  5.5 1.3 copy.41
  7.4 120.1 %forward.1 = (bf16[1536,1024]{1,0:T(8,128)(2,1)}, f32[4,512,128]{2,1,0:T(8,128)}, f32[4,1536,128]{2,1,0:T(8,128)}, bf16[4,1536,128]{2,1,0:T(8,128)(2,1)}, bf16[4...) custom-call(s32[6]{0:T(128)} %bitcast.71, ...), custom_call_target="tpu_custom_call" | custom-call | tf_op jit(solution)/shard_map/forward/pallas_call | solution.py:674
  127.5 20.8 %mlp.1 = (f32[2,256,1024]{2,1,0:T(8,128)}, bf16[2,256,1024]{2,1,0:T(8,128)(2,1)}, bf16[4,2,4,128,1024]{4,3,2,1,0:T(8,128)(2,1)}, f32[4,1,512]{2,1,0:T(1,128)}, f32[1,1024]{1,0:T(1,128)}) custom-call(bf16[512,1024]{1,0:T(8,128)(2,1)} %bitcast.58, bf16[512,1024]{1,0:T(8,128)(2,1)} %bitcast.59, bf16[4,2,4,128,1024]{4,3,2,1,0:T(8,128)(2,1)} %get-tuple-element.41.w_ref, ...), custom_call_target="tpu_custom_call" | custom-call | tf_op jit(solution)/shard_map/mlp/pallas_call | solution.py:791
  148.4 0.6 pad_convert_fusion.extra_ref
  149.0 164.7 %backward.1 = (bf16[256,1024]{1,0:T(8,128)(2,1)}, bf16[2,4,128,1024]{3,2,1,0:T(8,128)(2,1)}, bf16[512,1024]{1,0:T(8,128)(2,1)}, f32[256,1024]{1,0:T(8,128)}, f32[2,4,4,8,896]{4,3,2,1,0:T(8,128)}) custom-call(s32[6]{0:T(128)} %bitcast.72, f32[2,256,1024]{2,1,0:T(8,128)} %get-tuple-element.42.mine_ref, bf16[2,256,1024]{2,1,0:T(8,128)(2,1)} %get-tuple-element.43.theirs_ref, ...), custom_call_target="tpu_custom_call" | custom-call | tf_op jit(solution)/shard_map/backward/pallas_call | solution.py:1402
  313.7 1.7 fusion.10
  315.4 1.9 bitcast_convert_fusion
  317.3 1.8 copy.46
  319.8 0.6 reshape.81
  320.5 3.1 convolution_bitcast_fusion
  324.9 0.6 slice.69
  326.1 0.7 slice_reduce_fusion
  326.8 0.9 fusion.6
  327.7 0.6 copy.47
  328.4 1.4 copy.45
  329.8 0.8 slice_convert_fusion
  330.6 0.7 slice_reduce_fusion.2
  331.5 0.6 reduce_sum.38
  332.1 0.8 copy.69
  332.9 1.0 copy.70
  (28 shorter events, 3.3 us)
Async XLA Ops:
  0.6 4.9 %copy-start.2 = (bf16[1024,512]{1,0:T(8,128)(2,1)S(1)}, bf16[1024,512]{1,0:T(8,128)(2,1)}, u32[]{:S(2)}) copy-start(bf16[1024,512]{1,0:T(8,128)(2,1)} %param.29) | copy-start | bytes 3145732
  3.5 3.3 copy-start.7
  317.3 1.8 copy-start.4
  320.5 3.1 copy-start.6
  320.5 6.3 %copy-start = (bf16[128,6144]{1,0:T(8,128)(2,1)S(1)}, bf16[128,6144]{1,0:T(8,128)(2,1)}, u32[]{:S(2)}) copy-start(bf16[128,6144]{1,0:T(8,128)(2,1)} %ada_ref.1) | copy-start | bytes 4718596
  323.6 4.7 %copy-start.1 = (bf16[512,1024]{1,0:T(8,128)(2,1)S(1)}, bf16[512,1024]{1,0:T(8,128)(2,1)}, u32[]{:S(2)}) copy-start(bf16[512,1024]{1,0:T(8,128)(2,1)} %get-tuple-element.60) | copy-start | bytes 3145732
  328.3 3.8 %copy-start.5 = (bf16[256,1024]{1,0:T(8,128)(2,1)S(1)}, bf16[256,1024]{1,0:T(8,128)(2,1)}, u32[]{:S(2)}) copy-start(bf16[256,1024]{1,0:T(8,128)(2,1)} %get-tuple-element.118) | copy-start | bytes 1572868
  328.4 4.5 %copy-start.3 = (f32[256,1024]{1,0:T(8,128)S(1)}, f32[256,1024]{1,0:T(8,128)}, u32[]{:S(2)}) copy-start(f32[256,1024]{1,0:T(8,128)} %get-tuple-element.119) | copy-start | bytes 3145732
